TPU v7x, 128 devices: a whole 4x4x4 slice. The times are simulated.
128 devices in a mesh: row: 8 (over z, core), col: 16 (over y, x).
Axes of the slice: x: 4, y: 4, z: 4, core: 2. Of those that a mesh axis runs over, the one named last changes fastest.
Arguments:
- symmetric: float32 [16384, 16384], P('row', 'col'), may hold values from -8 to 8, as said below
- reflectors: float32 [4, 64, 16384], P(None, None, ('row', 'col')), may hold values from -0.125 to 0.125
- tri_factor: float32 [4, 64, 64], replicated, may hold values from -0.4 to 1.5, as said below
Outputs:
- updated: float32 [16384, 16384], P('row', 'col')
Inputs may be any that keep to these rules, and one draw needn't show every extreme that they name: symmetric is a symmetric matrix. Each tri_factor[p] is upper triangular.
All inputs are finite; a program needn't handle non-finite values.
Results may differ from a plain program's by a relative error of at most 0.00029.
Values sent between devices are 32-bit elements; how exact they have to be, the bound alone decides.
A program may use at most 64 MiB of HBM per device.

v0:
```python
import jax
import jax.numpy as jnp
from jax import lax
from jax.sharding import PartitionSpec as P


def broadcast(value, axis, source):
    kept = jnp.where(lax.axis_index(axis) == source, value, 0).astype(value.dtype)
    return lax.psum(kept, axis)


def shards(symmetric, reflectors, tri_factor):
    highest = lax.Precision.HIGHEST
    cols_here = symmetric.shape[1]
    row_count = lax.axis_size("row")
    col_count = lax.axis_size("col")
    col_index = lax.axis_index("col")
    owner = col_index * row_count // col_count
    offset = col_index % (col_count // row_count) * cols_here
    matrix = symmetric
    for panel in range(reflectors.shape[0]):
        piece = reflectors[panel]
        factor = tri_factor[panel]
        reflect_rows = lax.all_gather(piece, "col", axis=1, tiled=True)
        reflect_cols = broadcast(
            lax.dynamic_slice_in_dim(reflect_rows, offset, cols_here, 1), "row", owner
        )
        partial_value = lax.dot_general(
            reflect_cols,
            matrix,
            (((1,), (1,)), ((), ())),
            precision=highest,
            preferred_element_type=jnp.float32,
        )
        product_rows = lax.psum(partial_value, "col")
        image_rows = jnp.dot(
            factor.T, product_rows, precision=highest, preferred_element_type=jnp.float32
        )
        local_inner = lax.dot_general(
            reflect_rows,
            image_rows,
            (((1,), (1,)), ((), ())),
            precision=highest,
            preferred_element_type=jnp.float32,
        )
        inner = lax.psum(local_inner, "row")
        coupling = jnp.dot(factor.T, inner, precision=highest, preferred_element_type=jnp.float32)
        update_rows = image_rows - 0.5 * jnp.dot(
            coupling.T, reflect_rows, precision=highest, preferred_element_type=jnp.float32
        )
        update_cols = broadcast(
            lax.dynamic_slice_in_dim(update_rows, offset, cols_here, 1), "row", owner
        )
        left_block = jnp.concatenate([reflect_rows, update_rows], axis=0)
        right_block = jnp.concatenate([update_cols, reflect_cols], axis=0)
        matrix = matrix - lax.dot_general(
            left_block,
            right_block,
            (((0,), (0,)), ((), ())),
            precision=highest,
            preferred_element_type=jnp.float32,
        )
    return matrix


def solution(mesh):
    placed = (P("row", "col"), P(None, None, ("row", "col")), P())
    return jax.shard_map(
        shards, mesh=mesh, in_specs=placed, out_specs=P("row", "col"), check_vma=False
    )
```

profile of v0, /device:TPU:1, one launch (start us, length us, event | category | flops | bytes accessed | tf_op | source)
XLA Modules:
  0.0 877.3 jit_solution(7771888216284126579)
XLA Ops:
  7.4 20.3 %all-gather = f32[1,64,2048]{2,1,0:T(8,128)S(1)} all-gather(f32[1,64,128]{2,1,0:T(8,128)S(1)} %get-tuple-element.13), channel_id=2, replica_groups=mesh['row'=8,'col'=16] {'col'}, dimensions={2}, use_global_device_ids=true | all-gather | bytes 557056 | tf_op jit(solution)/shard_map/all_gather | solution.py:24
  28.5 63.6 %all-reduce.13.cloned.1.call-done = f32[64,1024]{1,0:T(8,128)} async-done(((f32[64,1024]{1,0:T(8,128)}), f32[64,1024]{1,0:T(8,128)}) %all-reduce.13.cloned.1.call-update) | async-done | bytes 262160 | tf_op jit(solution)/shard_map/psum | solution.py:9
  92.1 12.3 %fusion.65 = f32[64,2048]{1,0:T(8,128)} fusion(f32[64,1024]{1,0:T(8,128)} %all-reduce.13.cloned.1.call-done, f32[2048,1024]{1,0:T(8,128)} %param.3), kind=kOutput, calls=%fused_computation.85 | convolution fusion | flops 1610612736 | bytes 9175040 | tf_op jit(solution)/shard_map/dot_general | solution.py:28
  104.4 20.4 %all-gather.1 = f32[1,64,2048]{2,1,0:T(8,128)S(1)} all-gather(f32[1,64,128]{2,1,0:T(8,128)S(1)} %get-tuple-element.12), channel_id=3, replica_groups=mesh['row'=8,'col'=16] {'col'}, dimensions={2}, use_global_device_ids=true | all-gather | bytes 557056 | tf_op jit(solution)/shard_map/all_gather | solution.py:24
  125.6 63.7 %all-reduce.15.cloned.1.call-done = f32[64,2048]{1,0:T(8,128)} async-done(((f32[64,2048]{1,0:T(8,128)}), f32[64,2048]{1,0:T(8,128)}) %all-reduce.15.cloned.1.call-update) | async-done | bytes 524304 | tf_op jit(solution)/shard_map/psum | solution.py:35
  191.5 22.9 %psum.114 = f32[64,64]{0,1:T(8,128)S(1)} all-reduce(f32[64,64]{0,1:T(8,128)S(1)} %convolution_bitcast_fusion.3), channel_id=1, replica_groups=mesh['row'=8,'col'=16] {'row'}, use_global_device_ids=true, to_apply=%region_2.3 | all-reduce | flops 4096 | bytes 32768 | tf_op jit(solution)/shard_map/psum | solution.py:46
  216.2 58.2 %all-reduce.29.cloned.1.call-done = (f32[64,1024]{1,0:T(8,128)}, f32[64,1024]{1,0:T(8,128)}) async-done(((f32[64,1024]{1,0:T(8,128)}, f32[64,1024]{1,0:T(8,128)}), (f32[64,1024]{1,0:T(8,128)}, f32[64,1024]{1,0:T(8,128)})) %all-reduce.29.cloned.1.call-update) | async-done | bytes 524304 | tf_op jit(solution)/shard_map/psum | solution.py:9
  274.3 12.9 %convolution_subtract_fusion.3 = f32[2048,1024]{1,0:T(8,128)S(1)} fusion(f32[2048,1024]{1,0:T(8,128)} %param.3, f32[64,2048]{1,0:T(8,128)S(1)} %fusion.3, f32[64,2048]{1,0:T(8,128)S(1)} %bitcast.91, f32[64,1024]{1,0:T(8,128)S(1)} %copy-done.6, f32[64,1024]{1,0:T(8,128)} %get-tuple-element.9), kind=kOutput, calls=%fused_computation.3 | convolution fusion | flops 3223715840 | bytes 18350080 | tf_op jit(solution)/shard_map/dot_general | solution.py:56
  290.6 8.9 %fusion.66 = f32[64,2048]{1,0:T(8,128)} fusion(f32[64,1024]{1,0:T(8,128)S(1)} %copy-done.4, f32[2048,1024]{1,0:T(8,128)S(1)} %convolution_subtract_fusion.3), kind=kOutput, calls=%fused_computation.86 | convolution fusion | flops 1610612736 | bytes 9175040 | tf_op jit(solution)/shard_map/dot_general | solution.py:28
  299.6 20.6 %all-gather.2 = f32[1,64,2048]{2,1,0:T(8,128)S(1)} all-gather(f32[1,64,128]{2,1,0:T(8,128)S(1)} %get-tuple-element.14), channel_id=4, replica_groups=mesh['row'=8,'col'=16] {'col'}, dimensions={2}, use_global_device_ids=true | all-gather | bytes 557056 | tf_op jit(solution)/shard_map/all_gather | solution.py:24
  320.9 63.7 %all-reduce.17.cloned.1.call-done = f32[64,2048]{1,0:T(8,128)} async-done(((f32[64,2048]{1,0:T(8,128)}), f32[64,2048]{1,0:T(8,128)}) %all-reduce.17.cloned.1.call-update) | async-done | bytes 524304 | tf_op jit(solution)/shard_map/psum | solution.py:35
  386.8 22.9 %psum.118 = f32[64,64]{0,1:T(8,128)S(1)} all-reduce(f32[64,64]{0,1:T(8,128)S(1)} %convolution_bitcast_fusion.2), channel_id=1, replica_groups=mesh['row'=8,'col'=16] {'row'}, use_global_device_ids=true, to_apply=%region_6.7 | all-reduce | flops 4096 | bytes 32768 | tf_op jit(solution)/shard_map/psum | solution.py:46
  411.7 58.0 %all-reduce.27.cloned.1.call-done = (f32[64,1024]{1,0:T(8,128)}, f32[64,1024]{1,0:T(8,128)}) async-done(((f32[64,1024]{1,0:T(8,128)}, f32[64,1024]{1,0:T(8,128)}), (f32[64,1024]{1,0:T(8,128)}, f32[64,1024]{1,0:T(8,128)})) %all-reduce.27.cloned.1.call-update) | async-done | bytes 524304 | tf_op jit(solution)/shard_map/psum | solution.py:9
  469.8 12.9 %convolution_subtract_fusion.2 = f32[2048,1024]{1,0:T(8,128)S(1)} fusion(f32[2048,1024]{1,0:T(8,128)} %copy-done.1, f32[64,2048]{1,0:T(8,128)S(1)} %fusion.2, f32[64,2048]{1,0:T(8,128)S(1)} %bitcast.89, f32[64,1024]{1,0:T(8,128)S(1)} %copy-done.4, f32[64,1024]{1,0:T(8,128)} %get-tuple-element.7), kind=kOutput, calls=%fused_computation.2 | convolution fusion | flops 3223715840 | bytes 18350080 | tf_op jit(solution)/shard_map/dot_general | solution.py:56
  495.0 20.5 %all-gather.3 = f32[1,64,2048]{2,1,0:T(8,128)S(1)} all-gather(f32[1,64,128]{2,1,0:T(8,128)S(1)} %get-tuple-element.11), channel_id=5, replica_groups=mesh['row'=8,'col'=16] {'col'}, dimensions={2}, use_global_device_ids=true | all-gather | bytes 557056 | tf_op jit(solution)/shard_map/all_gather | solution.py:24
  516.3 63.7 %all-reduce.19.cloned.1.call-done = f32[64,2048]{1,0:T(8,128)} async-done(((f32[64,2048]{1,0:T(8,128)}), f32[64,2048]{1,0:T(8,128)}) %all-reduce.19.cloned.1.call-update) | async-done | bytes 524304 | tf_op jit(solution)/shard_map/psum | solution.py:35
  582.3 22.9 %psum.122 = f32[64,64]{0,1:T(8,128)S(1)} all-reduce(f32[64,64]{0,1:T(8,128)S(1)} %convolution_bitcast_fusion.1), channel_id=1, replica_groups=mesh['row'=8,'col'=16] {'row'}, use_global_device_ids=true, to_apply=%region_10.11 | all-reduce | flops 4096 | bytes 32768 | tf_op jit(solution)/shard_map/psum | solution.py:46
  606.9 58.2 %all-reduce.25.cloned.1.call-done = (f32[64,1024]{1,0:T(8,128)}, f32[64,1024]{1,0:T(8,128)}) async-done(((f32[64,1024]{1,0:T(8,128)}, f32[64,1024]{1,0:T(8,128)}), (f32[64,1024]{1,0:T(8,128)}, f32[64,1024]{1,0:T(8,128)})) %all-reduce.25.cloned.1.call-update) | async-done | bytes 524304 | tf_op jit(solution)/shard_map/psum | solution.py:9
  665.1 12.9 %convolution_subtract_fusion.1 = f32[2048,1024]{1,0:T(8,128)S(1)} fusion(f32[2048,1024]{1,0:T(8,128)} %copy-done, f32[64,2048]{1,0:T(8,128)S(1)} %fusion.1, f32[64,2048]{1,0:T(8,128)S(1)} %bitcast.88, f32[64,1024]{1,0:T(8,128)S(1)} %copy-done.3, f32[64,1024]{1,0:T(8,128)} %get-tuple-element.5), kind=kOutput, calls=%fused_computation.1 | convolution fusion | flops 3223715840 | bytes 18350080 | tf_op jit(solution)/shard_map/dot_general | solution.py:56
  681.4 8.9 %fusion.68 = f32[64,2048]{1,0:T(8,128)} fusion(f32[64,1024]{1,0:T(8,128)S(1)} %copy-done.5, f32[2048,1024]{1,0:T(8,128)S(1)} %convolution_subtract_fusion.1), kind=kOutput, calls=%fused_computation.88 | convolution fusion | flops 1610612736 | bytes 9175040 | tf_op jit(solution)/shard_map/dot_general | solution.py:28
  690.4 84.8 %all-reduce.21.cloned.1.call-done = f32[64,2048]{1,0:T(8,128)} async-done(((f32[64,2048]{1,0:T(8,128)}), f32[64,2048]{1,0:T(8,128)}) %all-reduce.21.cloned.1.call-update) | async-done | bytes 524304 | tf_op jit(solution)/shard_map/psum | solution.py:35
  777.4 23.3 %psum.126 = f32[64,64]{0,1:T(8,128)S(1)} all-reduce(f32[64,64]{0,1:T(8,128)S(1)} %convolution_bitcast_fusion), channel_id=1, replica_groups=mesh['row'=8,'col'=16] {'row'}, use_global_device_ids=true, to_apply=%region_14.15 | all-reduce | flops 4096 | bytes 32768 | tf_op jit(solution)/shard_map/psum | solution.py:46
  802.2 57.2 %all-reduce.23.cloned.1.call-done = f32[64,1024]{1,0:T(8,128)} async-done(((f32[64,1024]{1,0:T(8,128)}), f32[64,1024]{1,0:T(8,128)}) %all-reduce.23.cloned.1.call-update) | async-done | bytes 262160 | tf_op jit(solution)/shard_map/psum | solution.py:9
  859.4 11.2 %convolution_subtract_fusion = f32[2048,1024]{1,0:T(8,128)} fusion(f32[2048,1024]{1,0:T(8,128)} %copy-done.2, f32[64,2048]{1,0:T(8,128)S(1)} %fusion, f32[64,2048]{1,0:T(8,128)S(1)} %bitcast.90, f32[64,1024]{1,0:T(8,128)S(1)} %copy-done.5, f32[64,1024]{1,0:T(8,128)} %all-reduce.23.cloned.1.call-done), kind=kOutput, calls=%fused_computation | convolution fusion | flops 3223715840 | bytes 18350080 | tf_op jit(solution)/shard_map/dot_general | solution.py:56
  (60 shorter events, 38.8 us)
Async XLA Ops:
  6.5 182.7 %copy-start.7 = (f32[4,64,64]{2,1,0:T(8,128)S(1)}, f32[4,64,64]{2,1,0:T(8,128)}, u32[]{:S(2)}) copy-start(f32[4,64,64]{2,1,0:T(8,128)} %param.5) | copy-start | bytes 196612
  6.5 85.5 %all-reduce.13.cloned.1.call-start = ((), (), s32[]{:S(2)}) async-start(), calls=%async_computation | async-start | bytes 524288 | tf_op jit(solution)/shard_map/psum | solution.py:9
  28.4 160.8 %all-reduce.15.cloned.1.call-start = ((), (), s32[]{:S(2)}) async-start(), calls=%async_computation.1 | async-start | bytes 1048576 | tf_op jit(solution)/shard_map/psum | solution.py:35
  92.1 182.3 %copy-start.6 = (f32[64,1024]{1,0:T(8,128)S(1)}, f32[64,1024]{1,0:T(8,128)}, u32[]{:S(2)}) copy-start(f32[64,1024]{1,0:T(8,128)} %all-reduce.13.cloned.1.call-done) | copy-start | bytes 786436
  104.4 170.0 %all-reduce.29.cloned.1.call-start = ((), (), s32[]{:S(2)}) async-start(), calls=%async_computation.8 | async-start | bytes 1048576 | tf_op jit(solution)/shard_map/psum | solution.py:9
  215.9 168.7 %all-reduce.17.cloned.1.call-start = ((), (), s32[]{:S(2)}) async-start(), calls=%async_computation.2 | async-start | bytes 1048576 | tf_op jit(solution)/shard_map/psum | solution.py:35
  274.3 16.3 %copy-start.4 = (f32[64,1024]{1,0:T(8,128)S(1)}, f32[64,1024]{1,0:T(8,128)}, u32[]{:S(2)}) copy-start(f32[64,1024]{1,0:T(8,128)} %get-tuple-element.10) | copy-start | bytes 786436
  287.2 3.4 copy-start.1
  299.6 170.2 %all-reduce.27.cloned.1.call-start = ((), (), s32[]{:S(2)}) async-start(), calls=%async_computation.7 | async-start | bytes 1048576 | tf_op jit(solution)/shard_map/psum | solution.py:9
  411.3 168.7 %all-reduce.19.cloned.1.call-start = ((), (), s32[]{:S(2)}) async-start(), calls=%async_computation.3 | async-start | bytes 1048576 | tf_op jit(solution)/shard_map/psum | solution.py:35
  469.8 16.3 %copy-start.3 = (f32[64,1024]{1,0:T(8,128)S(1)}, f32[64,1024]{1,0:T(8,128)}, u32[]{:S(2)}) copy-start(f32[64,1024]{1,0:T(8,128)} %get-tuple-element.8) | copy-start | bytes 786436
  482.7 3.4 copy-start
  495.0 170.1 %all-reduce.25.cloned.1.call-start = ((), (), s32[]{:S(2)}) async-start(), calls=%async_computation.6 | async-start | bytes 1048576 | tf_op jit(solution)/shard_map/psum | solution.py:9
  606.7 168.5 %all-reduce.21.cloned.1.call-start = ((), (), s32[]{:S(2)}) async-start(), calls=%async_computation.4 | async-start | bytes 1048576 | tf_op jit(solution)/shard_map/psum | solution.py:35
  665.1 16.3 %copy-start.5 = (f32[64,1024]{1,0:T(8,128)S(1)}, f32[64,1024]{1,0:T(8,128)}, u32[]{:S(2)}) copy-start(f32[64,1024]{1,0:T(8,128)} %get-tuple-element.6) | copy-start | bytes 786436
  678.0 3.4 copy-start.2
  690.3 169.1 %all-reduce.23.cloned.1.call-start = ((), (), s32[]{:S(2)}) async-start(), calls=%async_computation.5 | async-start | bytes 524288 | tf_op jit(solution)/shard_map/psum | solution.py:9
Sparse Core Ops, SparseCore 0:
  28.5 63.4 all-reduce.12
  104.5 84.7 all-reduce.14
  216.1 58.2 all-reduce.28
  299.7 84.8 all-reduce.16
  411.4 58.3 all-reduce.26
  495.1 84.8 all-reduce.18
  606.8 58.2 all-reduce.24
  690.4 84.7 all-reduce.20
  802.3 57.0 all-reduce.22
where the time goes:
time: 886 us; the launch traced here: 877 us
  waiting for transfers between devices  571 us (64%)
  blocking collectives  174 us (20%)
  matrix products  101 us (11%)
  between operations  13.6 us (2%)
  local copies, waits for them, and re-layouts  11 us (1%)
    psum x5, waiting for transfers between devices, broadcast(): return lax.psum(kept, axis)  295 us
    psum x4, waiting for transfers between devices, shards(): product_rows = lax.psum(partial_value, 'col')  276 us
    psum x4, blocking collectives, shards(): inner = lax.psum(local_inner, 'row')  92.1 us
    all_gather x4, blocking collectives, shards(): reflect_rows = lax.all_gather(piece, 'col', axis=1, tiled=True)  81.8 us
    dot_general x4, matrix products, shards(): lax.dot_general(left_block, right_block, (((0,), (0,)), ((), ())), precis...  49.8 us
    dot_general x4, matrix products, shards(): lax.dot_general(reflect_cols, matrix, (((1,), (1,)), ((), ())), precision...  39 us
  transfers between devices with their start and end apart: 9, of which 9 were waited for; matrix products, arithmetic and copies ran while one was open for 0% of the time, Pallas kernels for 0%

commit v1 on v0

v1 whole, which is shorter than its diff:
```python
import functools

import jax
import jax.numpy as jnp
from jax import lax
from jax.experimental import pallas as pl
from jax.experimental.pallas import tpu as pltpu
from jax.sharding import PartitionSpec as P

MESH = pl.DeviceIdType.MESH
F32 = jnp.float32
BF16 = jnp.bfloat16
NN = (((1,), (0,)), ((), ()))
NT = (((1,), (1,)), ((), ()))
TN = (((0,), (0,)), ((), ()))


def split(value):
    high = value.astype(BF16)
    return high, (value - high.astype(F32)).astype(BF16)


def dot3(left, right, dims):
    (lh, ll), (rh, rl) = left, right
    dot = functools.partial(lax.dot_general, dimension_numbers=dims, preferred_element_type=F32)
    return dot(lh, rh) + dot(lh, rl) + dot(ll, rh)


def dotf(left, right, dims):
    return dot3(split(left), split(right), dims)


class Place:
    def __init__(self):
        row, col = lax.axis_index("row"), lax.axis_index("col")
        self.z, self.k = row // 2, lax.rem(row, 2)
        self.y, self.x = col // 4, lax.rem(col, 4)
        self.s = row

    def dev(self, z=None, k=None, y=None, x=None):
        z = self.z if z is None else z
        k = self.k if k is None else k
        y = self.y if y is None else y
        x = self.x if x is None else x
        return (z * 2 + k, y * 4 + x)

    def out_v(self):
        s = lax.rem(self.y, 2) * 4 + self.x
        return self.dev(s // 2, lax.rem(s, 2), self.z, self.k * 2 + self.y // 2), s

    def out_y(self):
        half = lax.rem(self.x, 2)
        b = half * 8 + self.s
        return self.dev(self.y, self.x // 2, b // 4, lax.rem(b, 4)), b


def wrap(value, by):
    return lax.rem(value + by + 4, 4)


class Ring:
    def __init__(self, ssem, rsem):
        self.ssem, self.rsem = ssem, rsem
        self.sent = []

    def copy(self, i, src, dst, dev):
        return pltpu.make_async_remote_copy(
            src_ref=src, dst_ref=dst, send_sem=self.ssem.at[i], recv_sem=self.rsem.at[i],
            device_id=dev, device_id_type=MESH)

    def send(self, i, src, dst, dev):
        c = self.copy(i, src, dst, dev)
        c.start()
        self.sent.append(c)

    def got(self, i, ref, dev):
        self.copy(i, ref, ref, dev).wait_recv()

    def drain(self):
        for c in self.sent:
            c.wait_send()
        self.sent = []


def plane_gather(pos, buf, ssem, rsem, hooks=()):
    ring = Ring(ssem, rsem)
    rows = buf.shape[1]
    half, quarter = rows // 2, rows // 4
    me = pos.dev()

    class Half:
        def __init__(self, h):
            self.h, self.base = h, h * 20
            self.i, self.j = (pos.x, pos.y) if h == 0 else (pos.y, pos.x)

        def at(self, di, dj, part=None):
            i, j = wrap(self.i, di), wrap(self.j, dj)
            slot = j * 4 + i if self.h == 0 else i * 4 + j
            if part is None:
                return buf.at[slot, pl.ds(self.h * half, half)]
            return buf.at[slot, pl.ds(self.h * half + part * quarter, quarter)]

        def first(self, d):
            return pos.dev(x=wrap(pos.x, d)) if self.h == 0 else pos.dev(y=wrap(pos.y, d))

        def second(self, d):
            return pos.dev(y=wrap(pos.y, d)) if self.h == 0 else pos.dev(x=wrap(pos.x, d))

        def send1(self):
            for n, d in ((0, 1), (1, -1)):
                ring.send(self.base + n, self.at(0, 0), self.at(0, 0), self.first(d))

        def relay1(self, n):
            d = (-1, 1)[n]
            ring.got(self.base + n, self.at(d, 0), me)
            ref = self.at(d, 0, n)
            ring.send(self.base + 2 + n, ref, ref, self.first(-d))

        def far1(self):
            for n in (0, 1):
                ring.got(self.base + 2 + n, self.at(2, 0, n), me)

        def send2(self, c):
            di = (0, -1, 1, 2)[c]
            for n, d in ((0, 1), (1, -1)):
                ring.send(self.base + 4 + 4 * c + n, self.at(di, 0), self.at(di, 0), self.second(d))

        def relay2(self, c):
            di = (0, -1, 1, 2)[c]
            for n, d in ((0, -1), (1, 1)):
                ring.got(self.base + 4 + 4 * c + n, self.at(di, d), me)
                ref = self.at(di, d, n)
                ring.send(self.base + 4 + 4 * c + 2 + n, ref, ref, self.second(-d))

        def far2(self, c):
            di = (0, -1, 1, 2)[c]
            for n in (0, 1):
                ring.got(self.base + 4 + 4 * c + 2 + n, self.at(di, 2, n), me)

    halves = (Half(0), Half(1))
    for h in halves:
        h.send1()
    for h in halves:
        h.send2(0)
    for h in halves:
        h.relay1(0)
        h.send2(1)
        h.relay1(1)
        h.send2(2)
    for hook in hooks:
        hook()
    for h in halves:
        h.relay2(0)
    for h in halves:
        h.far1()
        h.send2(3)
    for c in (1, 2, 3):
        for h in halves:
            h.relay2(c)
    for c in (0, 1, 2, 3):
        for h in halves:
            h.far2(c)
    return ring


class Column:
    def __init__(self, pos, buf, ssem, rsem):
        self.pos, self.buf = pos, buf
        self.ring = Ring(ssem, rsem)
        self.me = pos.dev()
        self.partner = pos.dev(k=1 - pos.k)
        self.quarter = buf.shape[1] // 2

    def at(self, dz, part=None, other=False):
        k = 1 - self.pos.k if other else self.pos.k
        slot = wrap(self.pos.z, dz) * 2 + k
        if part is None:
            return self.buf.at[slot]
        return self.buf.at[slot, pl.ds(part * self.quarter, self.quarter)]

    def zdev(self, d):
        return self.pos.dev(z=wrap(self.pos.z, d))

    def start(self):
        own = self.at(0)
        self.ring.send(0, own, own, self.zdev(1))
        self.ring.send(1, own, own, self.zdev(-1))
        self.ring.send(4, own, own, self.partner)

    def relay(self):
        for n, d in ((0, -1), (1, 1)):
            ref = self.at(d)
            self.ring.got(n, ref, self.me)
            part = self.at(d, n)
            self.ring.send(2 + n, part, part, self.zdev(-d))
            self.ring.send(5 + n, ref, ref, self.partner)

    def finish(self):
        for n in (0, 1):
            self.ring.got(2 + n, self.at(2, n), self.me)
        ref = self.at(2)
        self.ring.send(7, ref, ref, self.partner)
        for i, dz in ((4, 0), (5, -1), (6, 1), (7, 2)):
            self.ring.got(i, self.at(dz, other=True), self.me)


class Total:
    def __init__(self, pos, whole, out, part, in1, in2, in3, ssem, rsem):
        self.pos, self.whole, self.out, self.part = pos, whole, out, part
        self.ins = (in1, in2, in3)
        self.ring = Ring(ssem, rsem)
        self.me = pos.dev()
        self.rows = part.shape[0]

    def other(self, d):
        s = lax.rem(self.pos.s + d, 8)
        return s, self.pos.dev(s // 2, lax.rem(s, 2))

    def piece(self, s, ref=None):
        ref = self.whole if ref is None else ref
        return ref.at[pl.ds(pl.multiple_of(s * self.rows, self.rows), self.rows)]

    def step1(self):
        for d in range(1, 8):
            s, dev = self.other(d)
            self.ring.send(d - 1, self.piece(s), self.ins[0].at[d - 1], dev)

    def step2(self):
        value = self.piece(self.pos.s)[...]
        for d in range(7):
            self.ring.got(d, self.ins[0].at[d], self.me)
            value = value + self.ins[0][d]
        self.part[...] = value
        for d in (1, 2, 3):
            self.ring.send(6 + d, self.part, self.ins[1].at[d - 1], self.pos.dev(x=wrap(self.pos.x, d)))

    def step3(self):
        value = self.part[...]
        for d in (1, 2, 3):
            self.ring.got(6 + d, self.ins[1].at[d - 1], self.me)
            value = value + self.ins[1][d - 1]
        mid = self.ins[2].at[3]
        mid[...] = value
        for d in (1, 2, 3):
            self.ring.send(9 + d, mid, self.ins[2].at[d - 1], self.pos.dev(y=wrap(self.pos.y, d)))

    def step4(self):
        value = self.ins[2][3]
        for d in (1, 2, 3):
            self.ring.got(9 + d, self.ins[2].at[d - 1], self.me)
            value = value + self.ins[2][d - 1]
        own = self.piece(self.pos.s, self.out)
        own[...] = value
        for d in range(1, 8):
            _, dev = self.other(d)
            self.ring.send(12 + d, own, own, dev)

    def finish(self):
        for d in range(1, 8):
            s, _ = self.other(8 - d)
            self.ring.got(12 + d, self.piece(s, self.out), self.me)
        self.ring.drain()


def exchange(dev, me, src, dst, ssem, rsem):
    here = jnp.logical_and(dev[0] == me[0], dev[1] == me[1])
    remote = pltpu.make_async_remote_copy(
        src_ref=src, dst_ref=dst, send_sem=ssem, recv_sem=rsem, device_id=dev, device_id_type=MESH)

    @pl.when(here)
    def _():
        pltpu.make_async_copy(src, dst, rsem).start()

    @pl.when(jnp.logical_not(here))
    def _():
        remote.start()

    def drain():
        @pl.when(jnp.logical_not(here))
        def _():
            remote.wait_send()

    return drain


def gather_kernel(
    panels, a_hbm, v_ref, tri_ref,
    vth, vtl, yrows, zh, zl,
    a_mem, ah, al, vbuf, vh, vl, pbuf, cin, rin1, rin2, ytr, vcol, ycol, gpart, hpart, gmat, hmat, part,
    tin1, tin2, tin3, ct, dt,
    a_sem, vs, vr, ys, yr, vcs, vcr, ycs, ycr, gs, gr, hs, hr, cs, cr, zs, zr, ts, tr,
):
    pos = Place()
    me = pos.dev()
    nv, lanes = v_ref.shape
    nb = nv // panels
    rows, cols = a_mem.shape
    load = pltpu.make_async_copy(a_hbm, a_mem, a_sem)
    load.start()

    own_block = pos.y * 4 + pos.x
    vbuf[own_block] = v_ref[...]
    v_to, v_slot = pos.out_v()
    y_to, y_slot = pos.out_y()

    barrier = pltpu.get_barrier_semaphore()
    near = [pos.dev(x=wrap(pos.x, d)) for d in (1, 2, 3)]
    near += [pos.dev(y=wrap(pos.y, d)) for d in (1, 2, 3)]
    for d in range(1, 8):
        s = lax.rem(pos.s + d, 8)
        near.append(pos.dev(s // 2, lax.rem(s, 2)))
    near += [v_to, y_to]
    for dev in near:
        pl.semaphore_signal(barrier, inc=1, device_id=dev, device_id_type=MESH)
    pl.semaphore_wait(barrier, len(near))

    v_done = exchange(v_to, me, v_ref, vcol.at[v_slot], ts.at[0], tr.at[0])
    column_v = Column(pos, vcol, vcs, vcr)

    def column_start():
        own = vcol.at[pos.s]
        pltpu.make_async_copy(own, own, tr.at[0]).wait()
        column_v.start()

    gpart[...] = dotf(v_ref[...], v_ref[...], NT)
    total_g = Total(pos, gpart, gmat, part.at[0], tin1.at[0], tin2.at[0], tin3.at[0], gs, gr)

    ring_v = plane_gather(pos, vbuf, vs, vr, (total_g.step1, column_start))

    load.wait()

    @pl.loop(0, rows // lanes)
    def _(i):
        at = pl.ds(pl.multiple_of(i * lanes, lanes), lanes)
        ah[at], al[at] = split(a_mem[at])

    column_v.relay()
    total_g.step2()
    for b in range(16):
        high, low = split(vbuf[b])
        vh[:, b * lanes:(b + 1) * lanes] = high
        vl[:, b * lanes:(b + 1) * lanes] = low
    total_g.step3()
    column_v.finish()
    total_g.step4()

    @pl.loop(0, cols // (2 * lanes))
    def _(n):
        at = pl.ds(pl.multiple_of(n * 2 * lanes, 2 * lanes), 2 * lanes)
        value = dot3((vh[...], vl[...]), (ah[:, at], al[:, at]), NN)
        pbuf[n * 2] = value[:, :lanes]
        pbuf[n * 2 + 1] = value[:, lanes:]

    ring_c = Ring(cs, cr)
    partner = pos.dev(k=1 - pos.k)
    for q in range(4):
        ring_c.send(q, pbuf.at[2 * q + 1 - pos.k], cin.at[q], partner)

    acc = dotf(vcol[0], pbuf[0], NT)
    for s in range(1, 8):
        acc = acc + dotf(vcol[s], pbuf[s], NT)
    hpart[...] = acc
    total_h = Total(pos, hpart, hmat, part.at[1], tin1.at[1], tin2.at[1], tin3.at[1], hs, hr)
    total_h.step1()

    for q in range(4):
        ring_c.got(q, cin.at[q], me)
        mine = pbuf.at[2 * q + pos.k]
        cin[q] = cin[q] + mine[...]
    ring_z = Ring(zs, zr)
    half = nv // 2
    far, right, left = wrap(pos.z, 2), wrap(pos.z, 1), wrap(pos.z, -1)
    ring_z.send(0, cin.at[far, pl.ds(0, half)], rin1.at[0], pos.dev(z=right))
    ring_z.send(1, cin.at[far, pl.ds(half, half)], rin1.at[1], pos.dev(z=left))
    for n, to in ((0, right), (1, left)):
        ring_z.got(n, rin1.at[n], me)
        at = cin.at[to, pl.ds(n * half, half)]
        at[...] = at[...] + rin1[n]
        ring_z.send(2 + n, cin.at[to], rin2.at[n], pos.dev(z=to))
    total_h.step2()
    for n in (0, 1):
        ring_z.got(2 + n, rin2.at[n], me)
    shard = cin[pos.z] + rin2[0] + rin2[1]
    ycol[pos.s] = shard
    ytr[...] = shard.T
    y_done = exchange(y_to, me, ytr, yrows.at[y_slot], ts.at[1], tr.at[1])
    column_y = Column(pos, ycol, ycs, ycr)
    column_y.start()
    total_h.step3()
    pltpu.make_async_copy(ytr, yrows.at[own_block], tr.at[1]).wait()

    def middle():
        column_y.relay()
        total_h.step4()

    ring_y = plane_gather(pos, yrows, ys, yr, (middle,))
    column_y.finish()
    total_g.finish()
    total_h.finish()

    ct[...] = jnp.zeros_like(ct)
    dt[...] = jnp.zeros_like(dt)
    for p in range(panels):
        at = pl.ds(p * nb, nb)
        factor = split(tri_ref[p])
        pick = (lax.broadcasted_iota(jnp.int32, (nb, nv), 1)
                == lax.broadcasted_iota(jnp.int32, (nb, nv), 0) + p * nb).astype(F32)
        gp, hp = split(gmat[at]), split(hmat[at])
        c_all, d_all = split(ct[...]), split(dt[...])
        pc = pick - dot3(gp, c_all, NN)
        pd = -(dot3(hp, c_all, NT) + dot3(gp, d_all, NT) + dot3(gp, d_all, NN))
        ic, idt = dot3(factor, split(pc), TN), dot3(factor, split(pd), TN)
        inner = dot3(split(ic), hp, NT) + dot3(split(idt), gp, NT)
        coupling = dot3(split(inner), factor, NN)
        ct[at] = ic
        dt[at] = idt - 0.5 * dotf(coupling, pick, NN)
    c_pair = split(ct[...])
    ct_pair = split(ct[...].T)
    d_pair = split(dt[...] + dt[...].T)
    for s in range(8):
        at = slice(s * lanes, (s + 1) * lanes)
        vc, yc = split(vcol[s]), split(ycol[s])
        high, low = split(dot3(d_pair, vc, NN) + dot3(c_pair, yc, NN))
        zh[:nv, at], zl[:nv, at] = high, low
        high, low = split(dot3(ct_pair, vc, NN))
        zh[nv:, at], zl[nv:, at] = high, low

    @pl.loop(0, 16)
    def _(b):
        at = pl.ds(pl.multiple_of(b * lanes, lanes), lanes)
        vth[at], vtl[at] = split(vbuf[b].T)

    v_done()
    y_done()
    for ring in (ring_v, ring_c, ring_z, ring_y, column_v.ring, column_y.ring):
        ring.drain()


def update_kernel(a_ref, vth, vtl, y_ref, zh, zl, out_ref):
    nv = y_ref.shape[1]
    yh, yl = split(y_ref[...])
    z1 = (zh[:nv], zl[:nv])
    z2 = (zh[nv:], zl[nv:])
    out_ref[...] = a_ref[...] - (dot3((vth[...], vtl[...]), z1, NN) + dot3((yh, yl), z2, NN))


def shards(symmetric, reflectors, tri_factor):
    panels, nb, lanes = reflectors.shape
    nv = panels * nb
    rows, cols = symmetric.shape
    vmem = pl.BlockSpec(memory_space=pltpu.VMEM)
    dma = pltpu.SemaphoreType.DMA
    shape = jax.ShapeDtypeStruct
    vth, vtl, yrows, zh, zl = pl.pallas_call(
        functools.partial(gather_kernel, panels),
        out_shape=(
            shape((rows, nv), BF16), shape((rows, nv), BF16),
            shape((16, lanes, nv), F32),
            shape((2 * nv, cols), BF16), shape((2 * nv, cols), BF16),
        ),
        in_specs=[pl.BlockSpec(memory_space=pl.ANY), vmem, vmem],
        out_specs=(vmem,) * 5,
        scratch_shapes=[
            pltpu.VMEM((rows, cols), F32),
            pltpu.VMEM((rows, cols), BF16), pltpu.VMEM((rows, cols), BF16),
            pltpu.VMEM((16, nv, lanes), F32),
            pltpu.VMEM((nv, rows), BF16), pltpu.VMEM((nv, rows), BF16),
            pltpu.VMEM((8, nv, lanes), F32),
            pltpu.VMEM((4, nv, lanes), F32),
            pltpu.VMEM((2, nv // 2, lanes), F32),
            pltpu.VMEM((2, nv, lanes), F32),
            pltpu.VMEM((lanes, nv), F32),
            pltpu.VMEM((8, nv, lanes), F32), pltpu.VMEM((8, nv, lanes), F32),
            pltpu.VMEM((nv, nv), F32), pltpu.VMEM((nv, nv), F32),
            pltpu.VMEM((nv, nv), F32), pltpu.VMEM((nv, nv), F32),
            pltpu.VMEM((2, nv // 8, nv), F32),
            pltpu.VMEM((2, 7, nv // 8, nv), F32),
            pltpu.VMEM((2, 3, nv // 8, nv), F32),
            pltpu.VMEM((2, 4, nv // 8, nv), F32),
            pltpu.VMEM((nv, nv), F32), pltpu.VMEM((nv, nv), F32),
            dma, dma((40,)), dma((40,)), dma((40,)), dma((40,)),
            dma((8,)), dma((8,)), dma((8,)), dma((8,)),
            dma((20,)), dma((20,)), dma((20,)), dma((20,)),
            dma((4,)), dma((4,)), dma((4,)), dma((4,)), dma((2,)), dma((2,)),
        ],
        compiler_params=pltpu.CompilerParams(
            collective_id=0, has_side_effects=True, vmem_limit_bytes=56 * 2**20),
    )(symmetric, reflectors.reshape(nv, lanes), tri_factor)
    tile = 2 * lanes
    return pl.pallas_call(
        update_kernel,
        grid=(rows // tile,),
        out_shape=shape((rows, cols), F32),
        in_specs=[
            pl.BlockSpec((tile, cols), lambda i: (i, 0)),
            pl.BlockSpec((tile, nv), lambda i: (i, 0)),
            pl.BlockSpec((tile, nv), lambda i: (i, 0)),
            pl.BlockSpec((tile, nv), lambda i: (i, 0)),
            pl.BlockSpec((2 * nv, cols), lambda i: (0, 0)),
            pl.BlockSpec((2 * nv, cols), lambda i: (0, 0)),
        ],
        out_specs=pl.BlockSpec((tile, cols), lambda i: (i, 0)),
        compiler_params=pltpu.CompilerParams(vmem_limit_bytes=40 * 2**20),
    )(symmetric, vth, vtl, yrows.reshape(rows, nv), zh, zl)


def solution(mesh):
    placed = (P("row", "col"), P(None, None, ("row", "col")), P())
    return jax.shard_map(
        shards, mesh=mesh, in_specs=placed, out_specs=P("row", "col"), check_vma=False
    )
```

time: 886 us -> 120 us (0.14)
  the two profiles are of different devices: /device:TPU:1 before, /device:TPU:35 now
where the time goes in v1:
time: 120 us
  Pallas kernels  113 us (94%)
  local copies, waits for them, and re-layouts  6.48 us (5%)
    pallas_call x1, Pallas kernels, shards(): pl.pallas_call(functools.partial(gather_kernel, panels), out_shape=(shape...  101 us
    pallas_call x1, Pallas kernels, shards(): pl.pallas_call(update_kernel, grid=(rows // tile,), out_shape=shape((rows...  12.2 us
    unnamed x10, local copies, waits for them, and re-layouts  6.48 us

profile of v1, /device:TPU:35, one launch (start us, length us, event | category | flops | bytes accessed | tf_op | source)
XLA Modules:
  0.0 119.8 jit_solution(12422703525251807843)
XLA Ops:
  0.0 101.1 %shard_map.37 = (bf16[2048,256]{1,0:T(8,128)(2,1)}, bf16[2048,256]{1,0:T(8,128)(2,1)}, f32[16,128,256]{2,1,0:T(8,128)}, bf16[512,1024]{1,0:T(8,128)(2,1)}, bf16[512,1024]{1,0:T(8,128)(2,1)}) custom-call(f32[2048,1024]{1,0:T(8,128)} %a_ref.1, f32[256,128]{1,0:T(8,128)} %bitcast.3, f32[4,64,64]{2,1,0:T(8,128)} %tri_ref.1), custom_call_target="tpu_custom_call" | custom-call | tf_op jit(solution)/shard_map/pallas_call | solution.py:454
  101.1 0.0 copy-start
  101.1 1.6 %copy-done = f32[16,128,256]{2,1,0:T(8,128)S(1)} copy-done((f32[16,128,256]{2,1,0:T(8,128)S(1)}, f32[16,128,256]{2,1,0:T(8,128)}, u32[]{:S(2)}) %copy-start) | copy-done | bytes 2097176
  102.7 0.0 copy-start.1
  102.7 1.2 %copy-done.1 = bf16[2048,256]{1,0:T(8,128)(2,1)S(1)} copy-done((bf16[2048,256]{1,0:T(8,128)(2,1)S(1)}, bf16[2048,256]{1,0:T(8,128)(2,1)}, u32[]{:S(2)}) %copy-start.1) | copy-done | bytes 1048600
  103.9 0.0 copy-start.2
  103.9 1.2 %copy-done.2 = bf16[2048,256]{1,0:T(8,128)(2,1)S(1)} copy-done((bf16[2048,256]{1,0:T(8,128)(2,1)S(1)}, bf16[2048,256]{1,0:T(8,128)(2,1)}, u32[]{:S(2)}) %copy-start.2) | copy-done | bytes 1048600
  105.1 0.0 copy-start.3
  105.1 1.2 %copy-done.3 = bf16[512,1024]{1,0:T(8,128)(2,1)S(1)} copy-done((bf16[512,1024]{1,0:T(8,128)(2,1)S(1)}, bf16[512,1024]{1,0:T(8,128)(2,1)}, u32[]{:S(2)}) %copy-start.3) | copy-done | bytes 1048600
  106.4 0.0 copy-start.4
  106.4 1.2 %copy-done.4 = bf16[512,1024]{1,0:T(8,128)(2,1)S(1)} copy-done((bf16[512,1024]{1,0:T(8,128)(2,1)S(1)}, bf16[512,1024]{1,0:T(8,128)(2,1)}, u32[]{:S(2)}) %copy-start.4) | copy-done | bytes 1048600
  107.6 12.2 %shard_map.38 = f32[2048,1024]{1,0:T(8,128)} custom-call(f32[2048,1024]{1,0:T(8,128)} %a_ref.1, bf16[2048,256]{1,0:T(8,128)(2,1)S(1)} %copy-done.1, bf16[2048,256]{1,0:T(8,128)(2,1)S(1)} %copy-done.2, f32[2048,256]{1,0:T(8,128)S(1)} %bitcast.2, bf16[512,1024]{1,0:T(8,128)(2,1)S(1)} %copy-done.3, bf16[512,1024]{1,0:T(8,128)(2,1)S(1)} %copy-done.4), custom_call_target="tpu_custom_call" | custom-call | tf_op jit(solution)/shard_map/pallas_call | solution.py:490
Async XLA Ops:
  101.1 1.6 %copy-start = (f32[16,128,256]{2,1,0:T(8,128)S(1)}, f32[16,128,256]{2,1,0:T(8,128)}, u32[]{:S(2)}) copy-start(f32[16,128,256]{2,1,0:T(8,128)} %get-tuple-element.12) | copy-start | bytes 6291460
  102.7 1.2 %copy-start.1 = (bf16[2048,256]{1,0:T(8,128)(2,1)S(1)}, bf16[2048,256]{1,0:T(8,128)(2,1)}, u32[]{:S(2)}) copy-start(bf16[2048,256]{1,0:T(8,128)(2,1)} %get-tuple-element.10.vth) | copy-start | bytes 3145732
  103.9 1.2 %copy-start.2 = (bf16[2048,256]{1,0:T(8,128)(2,1)S(1)}, bf16[2048,256]{1,0:T(8,128)(2,1)}, u32[]{:S(2)}) copy-start(bf16[2048,256]{1,0:T(8,128)(2,1)} %get-tuple-element.11.vtl) | copy-start | bytes 3145732
  105.1 1.2 %copy-start.3 = (bf16[512,1024]{1,0:T(8,128)(2,1)S(1)}, bf16[512,1024]{1,0:T(8,128)(2,1)}, u32[]{:S(2)}) copy-start(bf16[512,1024]{1,0:T(8,128)(2,1)} %get-tuple-element.13.zh) | copy-start | bytes 3145732
  106.4 1.2 %copy-start.4 = (bf16[512,1024]{1,0:T(8,128)(2,1)S(1)}, bf16[512,1024]{1,0:T(8,128)(2,1)}, u32[]{:S(2)}) copy-start(bf16[512,1024]{1,0:T(8,128)(2,1)} %get-tuple-element.14.zl) | copy-start | bytes 3145732

commit v2 on v1

--- a/solution.py
+++ b/solution.py
@@ -49,9 +49,29 @@
         return self.dev(s // 2, lax.rem(s, 2), self.z, self.k * 2 + self.y // 2), s
 
     def out_y(self):
-        half = lax.rem(self.x, 2)
-        b = half * 8 + self.s
-        return self.dev(self.y, self.x // 2, b // 4, lax.rem(b, 4)), b
+        side = 2 * lax.rem(self.x, 2) - 1
+        x = lax.rem(self.x + side * self.k + 4, 4)
+        y = lax.rem(self.y + self.z + 2 * self.k, 4)
+        return self.dev(self.y, self.x // 2, y, x), y * 4 + x
+
+    def from_v(self):
+        b = lax.rem(self.x, 2) * 8 + self.s
+        return self.dev(self.y, self.x // 2, b // 4, lax.rem(b, 4))
+
+    def source(self, y, x):
+        d = lax.rem(x - 2 * self.k + 4, 4)
+        k = d // 2
+        right = jnp.where(jnp.logical_or(d == 1, d == 2), 1, 0)
+        z = lax.rem(y - self.z + 8 - 2 * k, 4)
+        return right, z, k
+
+    def from_y(self):
+        right, z, k = self.source(self.y, self.x)
+        return self.dev(z, k, self.z, 2 * self.k + right)
+
+    def block_of(self, y, x):
+        right, z, k = self.source(y, x)
+        return right * 8 + 2 * z + k
 
 
 def wrap(value, by):
@@ -82,7 +102,7 @@
         self.sent = []
 
 
-def plane_gather(pos, buf, ssem, rsem, hooks=()):
+def plane_gather(pos, buf, ssem, rsem, hooks=None):
     ring = Ring(ssem, rsem)
     rows = buf.shape[1]
     half, quarter = rows // 2, rows // 4
@@ -137,26 +157,30 @@
             for n in (0, 1):
                 ring.got(self.base + 4 + 4 * c + 2 + n, self.at(di, 2, n), me)
 
+    hooks = hooks or {}
+    hook = lambda n: [task() for task in hooks.get(n, ())]
     halves = (Half(0), Half(1))
     for h in halves:
         h.send1()
     for h in halves:
         h.send2(0)
-    for h in halves:
-        h.relay1(0)
-        h.send2(1)
-        h.relay1(1)
-        h.send2(2)
-    for hook in hooks:
-        hook()
+    hook(0)
+    for n in (0, 1):
+        for h in halves:
+            h.relay1(n)
+            h.send2(1 + n)
+    hook(1)
     for h in halves:
         h.relay2(0)
+    hook(2)
     for h in halves:
         h.far1()
         h.send2(3)
+    hook(3)
     for c in (1, 2, 3):
         for h in halves:
             h.relay2(c)
+        hook(3 + c)
     for c in (0, 1, 2, 3):
         for h in halves:
             h.far2(c)
@@ -283,12 +307,11 @@
     return drain
 
 
-def gather_kernel(
-    panels, a_hbm, v_ref, tri_ref,
-    vth, vtl, yrows, zh, zl,
-    a_mem, ah, al, vbuf, vh, vl, pbuf, cin, rin1, rin2, ytr, vcol, ycol, gpart, hpart, gmat, hmat, part,
-    tin1, tin2, tin3, ct, dt,
-    a_sem, vs, vr, ys, yr, vcs, vcr, ycs, ycr, gs, gr, hs, hr, cs, cr, zs, zr, ts, tr,
+def panel_kernel(
+    panels, a_hbm, v_ref, tri_ref, out_hbm,
+    a_mem, ah, al, vbuf, vh, vl, pbuf, cin, rin1, rin2, ytr, colbuf, yrows,
+    gpart, hpart, gmat, hmat, part, tin1, tin2, tin3, ct, dt, zh, zl,
+    a_sem, o_sem, vs, vr, ys, yr, cols_s, cols_r, gs, gr, hs, hr, cs, cr, zs, zr, ts, tr,
 ):
     pos = Place()
     me = pos.dev()
@@ -298,8 +321,7 @@
     load = pltpu.make_async_copy(a_hbm, a_mem, a_sem)
     load.start()
 
-    own_block = pos.y * 4 + pos.x
-    vbuf[own_block] = v_ref[...]
+    vbuf[pos.y * 4 + pos.x] = v_ref[...]
     v_to, v_slot = pos.out_v()
     y_to, y_slot = pos.out_y()
 
@@ -309,98 +331,93 @@
     for d in range(1, 8):
         s = lax.rem(pos.s + d, 8)
         near.append(pos.dev(s // 2, lax.rem(s, 2)))
-    near += [v_to, y_to]
+    near += [pos.from_v(), pos.from_y()]
     for dev in near:
         pl.semaphore_signal(barrier, inc=1, device_id=dev, device_id_type=MESH)
     pl.semaphore_wait(barrier, len(near))
 
-    v_done = exchange(v_to, me, v_ref, vcol.at[v_slot], ts.at[0], tr.at[0])
-    column_v = Column(pos, vcol, vcs, vcr)
-
-    def column_start():
-        own = vcol.at[pos.s]
-        pltpu.make_async_copy(own, own, tr.at[0]).wait()
-        column_v.start()
-
-    gpart[...] = dotf(v_ref[...], v_ref[...], NT)
     total_g = Total(pos, gpart, gmat, part.at[0], tin1.at[0], tin2.at[0], tin3.at[0], gs, gr)
 
-    ring_v = plane_gather(pos, vbuf, vs, vr, (total_g.step1, column_start))
-
-    load.wait()
-
-    @pl.loop(0, rows // lanes)
-    def _(i):
-        at = pl.ds(pl.multiple_of(i * lanes, lanes), lanes)
-        ah[at], al[at] = split(a_mem[at])
-
-    column_v.relay()
-    total_g.step2()
+    def gram():
+        gpart[...] = dotf(v_ref[...], v_ref[...], NT)
+        total_g.step1()
+
+    def pairs():
+        load.wait()
+
+        @pl.loop(0, rows // lanes)
+        def _(i):
+            at = pl.ds(pl.multiple_of(i * lanes, lanes), lanes)
+            ah[at], al[at] = split(a_mem[at])
+
+    ring_v = plane_gather(pos, vbuf, vs, vr, {
+        0: (gram,), 1: (pairs,), 3: (total_g.step2,), 5: (total_g.step3,)})
+    v_done = exchange(v_to, me, v_ref, colbuf.at[v_slot, pl.ds(0, nv)], ts.at[0], tr.at[0])
     for b in range(16):
         high, low = split(vbuf[b])
         vh[:, b * lanes:(b + 1) * lanes] = high
         vl[:, b * lanes:(b + 1) * lanes] = low
-    total_g.step3()
-    column_v.finish()
+
+    ring_c, ring_z = Ring(cs, cr), Ring(zs, zr)
+    partner = pos.dev(k=1 - pos.k)
+    half = nv // 2
+    far, right, left = wrap(pos.z, 2), wrap(pos.z, 1), wrap(pos.z, -1)
+    order = (far, right, left, pos.z)
+
+    def product(i):
+        at = pl.ds(pl.multiple_of(order[i] * 2 * lanes, 2 * lanes), 2 * lanes)
+        value = dot3((vh[...], vl[...]), (ah[:, at], al[:, at]), NN)
+        pbuf[2 * i] = value[:, :lanes]
+        pbuf[2 * i + 1] = value[:, lanes:]
+        ring_c.send(i, pbuf.at[2 * i + 1 - pos.k], cin.at[i], partner)
+
+    def merge(i):
+        ring_c.got(i, cin.at[i], me)
+        cin[i] = cin[i] + pbuf[2 * i + pos.k]
+
+    product(0)
+    product(1)
+    merge(0)
+    ring_z.send(0, cin.at[0, pl.ds(0, half)], rin1.at[0], pos.dev(z=right))
+    ring_z.send(1, cin.at[0, pl.ds(half, half)], rin1.at[1], pos.dev(z=left))
+    product(2)
+    product(3)
     total_g.step4()
-
-    @pl.loop(0, cols // (2 * lanes))
-    def _(n):
-        at = pl.ds(pl.multiple_of(n * 2 * lanes, 2 * lanes), 2 * lanes)
-        value = dot3((vh[...], vl[...]), (ah[:, at], al[:, at]), NN)
-        pbuf[n * 2] = value[:, :lanes]
-        pbuf[n * 2 + 1] = value[:, lanes:]
-
-    ring_c = Ring(cs, cr)
-    partner = pos.dev(k=1 - pos.k)
-    for q in range(4):
-        ring_c.send(q, pbuf.at[2 * q + 1 - pos.k], cin.at[q], partner)
-
-    acc = dotf(vcol[0], pbuf[0], NT)
-    for s in range(1, 8):
-        acc = acc + dotf(vcol[s], pbuf[s], NT)
-    hpart[...] = acc
+    for n, to in ((0, right), (1, left)):
+        merge(1 + n)
+        ring_z.got(n, rin1.at[n], me)
+        at = cin.at[1 + n, pl.ds(n * half, half)]
+        at[...] = at[...] + rin1[n]
+        ring_z.send(2 + n, cin.at[1 + n], rin2.at[n], pos.dev(z=to))
+    merge(3)
+    for n in (0, 1):
+        ring_z.got(2 + n, rin2.at[n], me)
+    shard = cin[3] + rin2[0] + rin2[1]
+    ytr[...] = shard.T
+    y_done = exchange(y_to, me, ytr, yrows.at[y_slot], ts.at[1], tr.at[1])
+    colbuf[pos.s, nv:] = shard
+
+    own_v = colbuf.at[pos.s, pl.ds(0, nv)]
+    pltpu.make_async_copy(own_v, own_v, tr.at[0]).wait()
+    hpart[...] = dotf(own_v[...], shard, NT)
     total_h = Total(pos, hpart, hmat, part.at[1], tin1.at[1], tin2.at[1], tin3.at[1], hs, hr)
     total_h.step1()
-
-    for q in range(4):
-        ring_c.got(q, cin.at[q], me)
-        mine = pbuf.at[2 * q + pos.k]
-        cin[q] = cin[q] + mine[...]
-    ring_z = Ring(zs, zr)
-    half = nv // 2
-    far, right, left = wrap(pos.z, 2), wrap(pos.z, 1), wrap(pos.z, -1)
-    ring_z.send(0, cin.at[far, pl.ds(0, half)], rin1.at[0], pos.dev(z=right))
-    ring_z.send(1, cin.at[far, pl.ds(half, half)], rin1.at[1], pos.dev(z=left))
-    for n, to in ((0, right), (1, left)):
-        ring_z.got(n, rin1.at[n], me)
-        at = cin.at[to, pl.ds(n * half, half)]
-        at[...] = at[...] + rin1[n]
-        ring_z.send(2 + n, cin.at[to], rin2.at[n], pos.dev(z=to))
+    column = Column(pos, colbuf, cols_s, cols_r)
+    column.start()
+
+    @pl.loop(0, 16)
+    def _(b):
+        at = pl.ds(pl.multiple_of(b * lanes, lanes), lanes)
+        ah[at, :nv], al[at, :nv] = split(vbuf[b].T)
+
     total_h.step2()
-    for n in (0, 1):
-        ring_z.got(2 + n, rin2.at[n], me)
-    shard = cin[pos.z] + rin2[0] + rin2[1]
-    ycol[pos.s] = shard
-    ytr[...] = shard.T
-    y_done = exchange(y_to, me, ytr, yrows.at[y_slot], ts.at[1], tr.at[1])
-    column_y = Column(pos, ycol, ycs, ycr)
-    column_y.start()
-    total_h.step3()
-    pltpu.make_async_copy(ytr, yrows.at[own_block], tr.at[1]).wait()
-
-    def middle():
-        column_y.relay()
-        total_h.step4()
-
-    ring_y = plane_gather(pos, yrows, ys, yr, (middle,))
-    column_y.finish()
-    total_g.finish()
-    total_h.finish()
+    own_y = yrows.at[pos.y * 4 + pos.x]
+    pltpu.make_async_copy(own_y, own_y, tr.at[1]).wait()
 
     ct[...] = jnp.zeros_like(ct)
     dt[...] = jnp.zeros_like(dt)
-    for p in range(panels):
+
+    def panel(p):
         at = pl.ds(p * nb, nb)
         factor = split(tri_ref[p])
         pick = (lax.broadcasted_iota(jnp.int32, (nb, nv), 1)
@@ -414,34 +431,69 @@
         coupling = dot3(split(inner), factor, NN)
         ct[at] = ic
         dt[at] = idt - 0.5 * dotf(coupling, pick, NN)
-    c_pair = split(ct[...])
-    ct_pair = split(ct[...].T)
-    d_pair = split(dt[...] + dt[...].T)
-    for s in range(8):
-        at = slice(s * lanes, (s + 1) * lanes)
-        vc, yc = split(vcol[s]), split(ycol[s])
-        high, low = split(dot3(d_pair, vc, NN) + dot3(c_pair, yc, NN))
-        zh[:nv, at], zl[:nv, at] = high, low
-        high, low = split(dot3(ct_pair, vc, NN))
-        zh[nv:, at], zl[nv:, at] = high, low
-
-    @pl.loop(0, 16)
-    def _(b):
+
+    def first_panels():
+        total_g.finish()
+        total_h.finish()
+        for p in range(panels // 2):
+            panel(p)
+
+    def last_panels():
+        for p in range(panels // 2, panels):
+            panel(p)
+
+    def right_side():
+        column.finish()
+        c_pair = split(ct[...])
+        ct_pair = split(ct[...].T)
+        d_pair = split(dt[...] + dt[...].T)
+        for s in range(8):
+            at = slice(s * lanes, (s + 1) * lanes)
+            vc, yc = split(colbuf[s, :nv]), split(colbuf[s, nv:])
+            high, low = split(dot3(d_pair, vc, NN) + dot3(c_pair, yc, NN))
+            zh[:nv, at], zl[:nv, at] = high, low
+            high, low = split(dot3(ct_pair, vc, NN))
+            zh[nv:, at], zl[nv:, at] = high, low
+
+    tall, wide = 4 * lanes, 2 * lanes
+
+    def reflector_part(lo, hi):
+        @pl.loop(lo, hi)
+        def _(g):
+            at = pl.ds(pl.multiple_of(g * tall, tall), tall)
+            left_pair = (ah[at, :nv], al[at, :nv])
+            for n in range(cols // wide):
+                to = slice(n * wide, (n + 1) * wide)
+                a_mem[at, to] = a_mem[at, to] - dot3(left_pair, (zh[:nv, to], zl[:nv, to]), NN)
+
+    ring_y = plane_gather(pos, yrows, ys, yr, {
+        0: (total_h.step3, column.relay), 1: (total_h.step4,),
+        3: (first_panels,), 4: (last_panels,), 5: (right_side,),
+        6: (lambda: reflector_part(0, rows // tall),)})
+
+    def written(b):
         at = pl.ds(pl.multiple_of(b * lanes, lanes), lanes)
-        vth[at], vtl[at] = split(vbuf[b].T)
+        return pltpu.make_async_copy(a_mem.at[at], out_hbm.at[at], o_sem.at[b])
+
+    @pl.loop(0, 4)
+    def _(g):
+        left_pair = split(yrows[pl.ds(g * 4, 4)].reshape(tall, nv))
+        for n in range(cols // wide):
+            to = slice(n * wide, (n + 1) * wide)
+            value = dot3(left_pair, (zh[nv:, to], zl[nv:, to]), NN)
+            for i in range(4):
+                b = pos.block_of(g, i)
+                at = pl.ds(pl.multiple_of(b * lanes, lanes), lanes)
+                a_mem[at, to] = a_mem[at, to] - value[i * lanes:(i + 1) * lanes]
+        for i in range(4):
+            written(pos.block_of(g, i)).start()
 
     v_done()
     y_done()
-    for ring in (ring_v, ring_c, ring_z, ring_y, column_v.ring, column_y.ring):
+    for ring in (ring_v, ring_c, ring_z, ring_y, column.ring):
         ring.drain()
-
-
-def update_kernel(a_ref, vth, vtl, y_ref, zh, zl, out_ref):
-    nv = y_ref.shape[1]
-    yh, yl = split(y_ref[...])
-    z1 = (zh[:nv], zl[:nv])
-    z2 = (zh[nv:], zl[nv:])
-    out_ref[...] = a_ref[...] - (dot3((vth[...], vtl[...]), z1, NN) + dot3((yh, yl), z2, NN))
+    for b in range(16):
+        written(b).wait()
 
 
 def shards(symmetric, reflectors, tri_factor):
@@ -449,17 +501,13 @@
     nv = panels * nb
     rows, cols = symmetric.shape
     vmem = pl.BlockSpec(memory_space=pltpu.VMEM)
+    anywhere = pl.BlockSpec(memory_space=pl.ANY)
     dma = pltpu.SemaphoreType.DMA
-    shape = jax.ShapeDtypeStruct
-    vth, vtl, yrows, zh, zl = pl.pallas_call(
-        functools.partial(gather_kernel, panels),
-        out_shape=(
-            shape((rows, nv), BF16), shape((rows, nv), BF16),
-            shape((16, lanes, nv), F32),
-            shape((2 * nv, cols), BF16), shape((2 * nv, cols), BF16),
-        ),
-        in_specs=[pl.BlockSpec(memory_space=pl.ANY), vmem, vmem],
-        out_specs=(vmem,) * 5,
+    return pl.pallas_call(
+        functools.partial(panel_kernel, panels),
+        out_shape=jax.ShapeDtypeStruct((rows, cols), F32),
+        in_specs=[anywhere, vmem, vmem],
+        out_specs=anywhere,
         scratch_shapes=[
             pltpu.VMEM((rows, cols), F32),
             pltpu.VMEM((rows, cols), BF16), pltpu.VMEM((rows, cols), BF16),
@@ -470,7 +518,8 @@
             pltpu.VMEM((2, nv // 2, lanes), F32),
             pltpu.VMEM((2, nv, lanes), F32),
             pltpu.VMEM((lanes, nv), F32),
-            pltpu.VMEM((8, nv, lanes), F32), pltpu.VMEM((8, nv, lanes), F32),
+            pltpu.VMEM((8, 2 * nv, lanes), F32),
+            pltpu.VMEM((16, lanes, nv), F32),
             pltpu.VMEM((nv, nv), F32), pltpu.VMEM((nv, nv), F32),
             pltpu.VMEM((nv, nv), F32), pltpu.VMEM((nv, nv), F32),
             pltpu.VMEM((2, nv // 8, nv), F32),
@@ -478,30 +527,15 @@
             pltpu.VMEM((2, 3, nv // 8, nv), F32),
             pltpu.VMEM((2, 4, nv // 8, nv), F32),
             pltpu.VMEM((nv, nv), F32), pltpu.VMEM((nv, nv), F32),
-            dma, dma((40,)), dma((40,)), dma((40,)), dma((40,)),
-            dma((8,)), dma((8,)), dma((8,)), dma((8,)),
+            pltpu.VMEM((2 * nv, cols), BF16), pltpu.VMEM((2 * nv, cols), BF16),
+            dma, dma((16,)), dma((40,)), dma((40,)), dma((40,)), dma((40,)),
+            dma((8,)), dma((8,)),
             dma((20,)), dma((20,)), dma((20,)), dma((20,)),
             dma((4,)), dma((4,)), dma((4,)), dma((4,)), dma((2,)), dma((2,)),
         ],
         compiler_params=pltpu.CompilerParams(
             collective_id=0, has_side_effects=True, vmem_limit_bytes=56 * 2**20),
     )(symmetric, reflectors.reshape(nv, lanes), tri_factor)
-    tile = 2 * lanes
-    return pl.pallas_call(
-        update_kernel,
-        grid=(rows // tile,),
-        out_shape=shape((rows, cols), F32),
-        in_specs=[
-            pl.BlockSpec((tile, cols), lambda i: (i, 0)),
-            pl.BlockSpec((tile, nv), lambda i: (i, 0)),
-            pl.BlockSpec((tile, nv), lambda i: (i, 0)),
-            pl.BlockSpec((tile, nv), lambda i: (i, 0)),
-            pl.BlockSpec((2 * nv, cols), lambda i: (0, 0)),
-            pl.BlockSpec((2 * nv, cols), lambda i: (0, 0)),
-        ],
-        out_specs=pl.BlockSpec((tile, cols), lambda i: (i, 0)),
-        compiler_params=pltpu.CompilerParams(vmem_limit_bytes=40 * 2**20),
-    )(symmetric, vth, vtl, yrows.reshape(rows, nv), zh, zl)
 
 
 def solution(mesh):

time: 120 us -> 103 us (0.86)
  the two profiles are of different devices: /device:TPU:35 before, /device:TPU:1 now
where the time goes in v2:
time: 103 us
  Pallas kernels  94.6 us (92%)
  local copies, waits for them, and re-layouts  8.44 us (8%)
    pallas_call x1, Pallas kernels, shards(): pl.pallas_call(functools.partial(panel_kernel, panels), out_shape=jax.Sha...  94.6 us
    unnamed x1, local copies, waits for them, and re-layouts  8.44 us

profile of v2, /device:TPU:1, one launch (start us, length us, event | category | flops | bytes accessed | tf_op | source)
XLA Modules:
  0.0 103.1 jit_solution(7344490173242083994)
XLA Ops:
  0.0 94.6 %shard_map.37 = f32[2048,1024]{1,0:T(8,128)} custom-call(f32[2048,1024]{1,0:T(8,128)} %a_hbm.1, f32[256,128]{1,0:T(8,128)} %bitcast.1, f32[4,64,64]{2,1,0:T(8,128)} %tri_ref.1), custom_call_target="tpu_custom_call" | custom-call | tf_op jit(solution)/shard_map/pallas_call | solution.py:506
  94.7 8.4 %copy.5 = f32[2048,1024]{1,0:T(8,128)} copy(f32[2048,1024]{1,0:T(8,128)} %shard_map.37) | data formatting | bytes 16777216

commit v3 on v2

--- a/solution.py
+++ b/solution.py
@@ -234,7 +234,6 @@
         self.ins = (in1, in2, in3)
         self.ring = Ring(ssem, rsem)
         self.me = pos.dev()
-        self.rows = part.shape[0]
 
     def other(self, d):
         s = lax.rem(self.pos.s + d, 8)
@@ -242,7 +241,7 @@
 
     def piece(self, s, ref=None):
         ref = self.whole if ref is None else ref
-        return ref.at[pl.ds(pl.multiple_of(s * self.rows, self.rows), self.rows)]
+        return ref.at[s]
 
     def step1(self):
         for d in range(1, 8):
@@ -308,10 +307,10 @@
 
 
 def panel_kernel(
-    panels, a_hbm, v_ref, tri_ref, out_hbm,
+    panels, a_hbm, v_ref, tri_ref, mid_hbm, y_hbm, zh_hbm, zl_hbm,
     a_mem, ah, al, vbuf, vh, vl, pbuf, cin, rin1, rin2, ytr, colbuf, yrows,
-    gpart, hpart, gmat, hmat, part, tin1, tin2, tin3, ct, dt, zh, zl,
-    a_sem, o_sem, vs, vr, ys, yr, cols_s, cols_r, gs, gr, hs, hr, cs, cr, zs, zr, ts, tr,
+    packed, summed, gmat, hmat, part, tin1, tin2, tin3, ct, dt, zh, zl, yzh, yzl,
+    a_sem, m_sem, o_sem, z_sem, vs, vr, ys, yr, cols_s, cols_r, hs, hr, cs, cr, zs, zr, ts, tr,
 ):
     pos = Place()
     me = pos.dev()
@@ -336,12 +335,6 @@
         pl.semaphore_signal(barrier, inc=1, device_id=dev, device_id_type=MESH)
     pl.semaphore_wait(barrier, len(near))
 
-    total_g = Total(pos, gpart, gmat, part.at[0], tin1.at[0], tin2.at[0], tin3.at[0], gs, gr)
-
-    def gram():
-        gpart[...] = dotf(v_ref[...], v_ref[...], NT)
-        total_g.step1()
-
     def pairs():
         load.wait()
 
@@ -350,8 +343,7 @@
             at = pl.ds(pl.multiple_of(i * lanes, lanes), lanes)
             ah[at], al[at] = split(a_mem[at])
 
-    ring_v = plane_gather(pos, vbuf, vs, vr, {
-        0: (gram,), 1: (pairs,), 3: (total_g.step2,), 5: (total_g.step3,)})
+    ring_v = plane_gather(pos, vbuf, vs, vr, {1: (pairs,)})
     v_done = exchange(v_to, me, v_ref, colbuf.at[v_slot, pl.ds(0, nv)], ts.at[0], tr.at[0])
     for b in range(16):
         high, low = split(vbuf[b])
@@ -382,7 +374,6 @@
     ring_z.send(1, cin.at[0, pl.ds(half, half)], rin1.at[1], pos.dev(z=left))
     product(2)
     product(3)
-    total_g.step4()
     for n, to in ((0, right), (1, left)):
         merge(1 + n)
         ring_z.got(n, rin1.at[n], me)
@@ -399,9 +390,16 @@
 
     own_v = colbuf.at[pos.s, pl.ds(0, nv)]
     pltpu.make_async_copy(own_v, own_v, tr.at[0]).wait()
-    hpart[...] = dotf(own_v[...], shard, NT)
-    total_h = Total(pos, hpart, hmat, part.at[1], tin1.at[1], tin2.at[1], tin3.at[1], hs, hr)
-    total_h.step1()
+    row = lax.broadcasted_iota(jnp.int32, (nv, nv), 0)
+    column_index = lax.broadcasted_iota(jnp.int32, (nv, nv), 1)
+    below, on = row >= column_index, row == column_index
+    group = nv // 8
+    gram = dotf(v_ref[...], v_ref[...], NT)
+    packed[:, group:] = jnp.zeros_like(packed[:, group:])
+    packed[:, :group] = jnp.where(below, dotf(own_v[...], shard, NT), gram).reshape(8, group, nv)
+    packed[0, group:group + 1] = jnp.sum(jnp.where(on, gram, 0.0), axis=0, keepdims=True)
+    total = Total(pos, packed, summed, part, tin1, tin2, tin3, hs, hr)
+    total.step1()
     column = Column(pos, colbuf, cols_s, cols_r)
     column.start()
 
@@ -410,7 +408,7 @@
         at = pl.ds(pl.multiple_of(b * lanes, lanes), lanes)
         ah[at, :nv], al[at, :nv] = split(vbuf[b].T)
 
-    total_h.step2()
+    total.step2()
     own_y = yrows.at[pos.y * 4 + pos.x]
     pltpu.make_async_copy(own_y, own_y, tr.at[1]).wait()
 
@@ -432,68 +430,72 @@
         ct[at] = ic
         dt[at] = idt - 0.5 * dotf(coupling, pick, NN)
 
-    def first_panels():
-        total_g.finish()
-        total_h.finish()
-        for p in range(panels // 2):
+    def inner_products():
+        total.finish()
+        both = summed[:, :group].reshape(nv, nv)
+        turned = both.T
+        hmat[...] = jnp.where(below, both, turned)
+        gmat[...] = jnp.where(on, summed[0, group:group + 1], jnp.where(below, turned, both))
+
+    def coefficients():
+        for p in range(panels):
             panel(p)
 
-    def last_panels():
-        for p in range(panels // 2, panels):
-            panel(p)
+    right_copies = (
+        pltpu.make_async_copy(yzh, zh_hbm, z_sem.at[0]), pltpu.make_async_copy(yzl, zl_hbm, z_sem.at[1]))
 
     def right_side():
-        column.finish()
         c_pair = split(ct[...])
         ct_pair = split(ct[...].T)
         d_pair = split(dt[...] + dt[...].T)
         for s in range(8):
             at = slice(s * lanes, (s + 1) * lanes)
             vc, yc = split(colbuf[s, :nv]), split(colbuf[s, nv:])
-            high, low = split(dot3(d_pair, vc, NN) + dot3(c_pair, yc, NN))
-            zh[:nv, at], zl[:nv, at] = high, low
-            high, low = split(dot3(ct_pair, vc, NN))
-            zh[nv:, at], zl[nv:, at] = high, low
+            zh[:, at], zl[:, at] = split(dot3(d_pair, vc, NN) + dot3(c_pair, yc, NN))
+            yzh[:, at], yzl[:, at] = split(dot3(ct_pair, vc, NN))
+        for copy in right_copies:
+            copy.start()
 
     tall, wide = 4 * lanes, 2 * lanes
 
-    def reflector_part(lo, hi):
-        @pl.loop(lo, hi)
+    def middle_copy(g):
+        at = pl.ds(pl.multiple_of(g * tall, tall), tall)
+        return pltpu.make_async_copy(a_mem.at[at], mid_hbm.at[at], m_sem.at[g])
+
+    def reflector_part():
+        @pl.loop(0, rows // tall)
         def _(g):
             at = pl.ds(pl.multiple_of(g * tall, tall), tall)
             left_pair = (ah[at, :nv], al[at, :nv])
             for n in range(cols // wide):
                 to = slice(n * wide, (n + 1) * wide)
-                a_mem[at, to] = a_mem[at, to] - dot3(left_pair, (zh[:nv, to], zl[:nv, to]), NN)
+                a_mem[at, to] = a_mem[at, to] - dot3(left_pair, (zh[:, to], zl[:, to]), NN)
+            middle_copy(g).start()
 
     ring_y = plane_gather(pos, yrows, ys, yr, {
-        0: (total_h.step3, column.relay), 1: (total_h.step4,),
-        3: (first_panels,), 4: (last_panels,), 5: (right_side,),
-        6: (lambda: reflector_part(0, rows // tall),)})
-
-    def written(b):
-        at = pl.ds(pl.multiple_of(b * lanes, lanes), lanes)
-        return pltpu.make_async_copy(a_mem.at[at], out_hbm.at[at], o_sem.at[b])
-
-    @pl.loop(0, 4)
-    def _(g):
-        left_pair = split(yrows[pl.ds(g * 4, 4)].reshape(tall, nv))
-        for n in range(cols // wide):
-            to = slice(n * wide, (n + 1) * wide)
-            value = dot3(left_pair, (zh[nv:, to], zl[nv:, to]), NN)
-            for i in range(4):
-                b = pos.block_of(g, i)
-                at = pl.ds(pl.multiple_of(b * lanes, lanes), lanes)
-                a_mem[at, to] = a_mem[at, to] - value[i * lanes:(i + 1) * lanes]
-        for i in range(4):
-            written(pos.block_of(g, i)).start()
-
+        0: (total.step3, column.relay), 2: (total.step4,),
+        6: (column.finish, inner_products, coefficients, right_side, reflector_part)})
+
+    def row_copy(slot):
+        b = pos.block_of(slot // 4, slot % 4)
+        return pltpu.make_async_copy(yrows.at[slot], y_hbm.at[b], o_sem.at[slot])
+
+    for slot in range(16):
+        row_copy(slot).start()
     v_done()
     y_done()
     for ring in (ring_v, ring_c, ring_z, ring_y, column.ring):
         ring.drain()
-    for b in range(16):
-        written(b).wait()
+    for copy in right_copies:
+        copy.wait()
+    for g in range(rows // tall):
+        middle_copy(g).wait()
+    for slot in range(16):
+        row_copy(slot).wait()
+
+
+def product_kernel(mid_ref, y_ref, zh, zl, out_ref):
+    out_ref[...] = mid_ref[...] - dot3(split(y_ref[...]), (zh[...], zl[...]), NN)
 
 
 def shards(symmetric, reflectors, tri_factor):
@@ -503,11 +505,14 @@
     vmem = pl.BlockSpec(memory_space=pltpu.VMEM)
     anywhere = pl.BlockSpec(memory_space=pl.ANY)
     dma = pltpu.SemaphoreType.DMA
-    return pl.pallas_call(
+    shape = jax.ShapeDtypeStruct
+    middle, y_rows, zh, zl = pl.pallas_call(
         functools.partial(panel_kernel, panels),
-        out_shape=jax.ShapeDtypeStruct((rows, cols), F32),
+        out_shape=(
+            shape((rows, cols), F32), shape((16, lanes, nv), F32),
+            shape((nv, cols), BF16), shape((nv, cols), BF16)),
         in_specs=[anywhere, vmem, vmem],
-        out_specs=anywhere,
+        out_specs=(anywhere,) * 4,
         scratch_shapes=[
             pltpu.VMEM((rows, cols), F32),
             pltpu.VMEM((rows, cols), BF16), pltpu.VMEM((rows, cols), BF16),
@@ -520,22 +525,37 @@
             pltpu.VMEM((lanes, nv), F32),
             pltpu.VMEM((8, 2 * nv, lanes), F32),
             pltpu.VMEM((16, lanes, nv), F32),
+            pltpu.VMEM((8, nv // 8 + 8, nv), F32), pltpu.VMEM((8, nv // 8 + 8, nv), F32),
             pltpu.VMEM((nv, nv), F32), pltpu.VMEM((nv, nv), F32),
+            pltpu.VMEM((nv // 8 + 8, nv), F32),
+            pltpu.VMEM((7, nv // 8 + 8, nv), F32),
+            pltpu.VMEM((3, nv // 8 + 8, nv), F32),
+            pltpu.VMEM((4, nv // 8 + 8, nv), F32),
             pltpu.VMEM((nv, nv), F32), pltpu.VMEM((nv, nv), F32),
-            pltpu.VMEM((2, nv // 8, nv), F32),
-            pltpu.VMEM((2, 7, nv // 8, nv), F32),
-            pltpu.VMEM((2, 3, nv // 8, nv), F32),
-            pltpu.VMEM((2, 4, nv // 8, nv), F32),
-            pltpu.VMEM((nv, nv), F32), pltpu.VMEM((nv, nv), F32),
-            pltpu.VMEM((2 * nv, cols), BF16), pltpu.VMEM((2 * nv, cols), BF16),
-            dma, dma((16,)), dma((40,)), dma((40,)), dma((40,)), dma((40,)),
-            dma((8,)), dma((8,)),
-            dma((20,)), dma((20,)), dma((20,)), dma((20,)),
+            pltpu.VMEM((nv, cols), BF16), pltpu.VMEM((nv, cols), BF16),
+            pltpu.VMEM((nv, cols), BF16), pltpu.VMEM((nv, cols), BF16),
+            dma, dma((4,)), dma((16,)), dma((2,)),
+            dma((40,)), dma((40,)), dma((40,)), dma((40,)),
+            dma((8,)), dma((8,)), dma((20,)), dma((20,)),
             dma((4,)), dma((4,)), dma((4,)), dma((4,)), dma((2,)), dma((2,)),
         ],
         compiler_params=pltpu.CompilerParams(
             collective_id=0, has_side_effects=True, vmem_limit_bytes=56 * 2**20),
     )(symmetric, reflectors.reshape(nv, lanes), tri_factor)
+    tile = 2 * lanes
+    return pl.pallas_call(
+        product_kernel,
+        grid=(rows // tile,),
+        out_shape=shape((rows, cols), F32),
+        in_specs=[
+            pl.BlockSpec((tile, cols), lambda i: (i, 0)),
+            pl.BlockSpec((tile, nv), lambda i: (i, 0)),
+            pl.BlockSpec((nv, cols), lambda i: (0, 0)),
+            pl.BlockSpec((nv, cols), lambda i: (0, 0)),
+        ],
+        out_specs=pl.BlockSpec((tile, cols), lambda i: (i, 0)),
+        compiler_params=pltpu.CompilerParams(vmem_limit_bytes=58 * 2**20),
+    )(middle, y_rows.reshape(rows, nv), zh, zl)
 
 
 def solution(mesh):

time: 103 us -> 92.5 us (0.90)
  local copies, waits for them, and re-layouts: 8.44 us -> 0 us
  Pallas kernels: 94.6 us -> 92.2 us
    unnamed x1 -> x0, local copies, waits for them, and re-layouts: 8.44 us -> none
    pallas_call x1 -> x2, Pallas kernels: 94.6 us -> 92.2 us  [the longest x1 80.6 us: shards(): pl.pallas_call(functools.partial(panel_kernel, panels), out_shape=(shape(...]
where the time goes in v3:
time: 92.5 us; the launch traced here: 92.2 us
  Pallas kernels  92.2 us (100%)
    pallas_call x1, Pallas kernels, shards(): pl.pallas_call(functools.partial(panel_kernel, panels), out_shape=(shape(...  80.6 us
    pallas_call x1, Pallas kernels, shards(): pl.pallas_call(product_kernel, grid=(rows // tile,), out_shape=shape((row...  11.6 us

profile of v3, /device:TPU:1, one launch (start us, length us, event | category | flops | bytes accessed | tf_op | source)
XLA Modules:
  0.0 92.2 jit_solution(6870111946709727752)
XLA Ops:
  0.0 80.6 %shard_map.37 = (f32[2048,1024]{1,0:T(8,128)}, f32[16,128,256]{2,1,0:T(8,128)}, bf16[256,1024]{1,0:T(8,128)(2,1)}, bf16[256,1024]{1,0:T(8,128)(2,1)}) custom-call(f32[2048,1024]{1,0:T(8,128)} %a_hbm.1, f32[256,128]{1,0:T(8,128)} %bitcast.3, f32[4,64,64]{2,1,0:T(8,128)} %tri_ref.1), custom_call_target="tpu_custom_call" | custom-call | tf_op jit(solution)/shard_map/pallas_call | solution.py:509
  80.6 11.6 %shard_map.38 = f32[2048,1024]{1,0:T(8,128)} custom-call(f32[2048,1024]{1,0:T(8,128)} %get-tuple-element.9.mid_ref, f32[2048,256]{1,0:T(8,128)} %bitcast.2, bf16[256,1024]{1,0:T(8,128)(2,1)} %get-tuple-element.11.zh, bf16[256,1024]{1,0:T(8,128)(2,1)} %get-tuple-element.12.zl), custom_call_target="tpu_custom_call" | custom-call | tf_op jit(solution)/shard_map/pallas_call | solution.py:546

commit v4 on v3

--- a/solution.py
+++ b/solution.py
@@ -107,6 +107,7 @@
     rows = buf.shape[1]
     half, quarter = rows // 2, rows // 4
     me = pos.dev()
+    direct = (3,)
 
     class Half:
         def __init__(self, h):
@@ -129,33 +130,36 @@
         def send1(self):
             for n, d in ((0, 1), (1, -1)):
                 ring.send(self.base + n, self.at(0, 0), self.at(0, 0), self.first(d))
+            ring.send(self.base + 2, self.at(0, 0), self.at(0, 0), self.first(2))
 
         def relay1(self, n):
             d = (-1, 1)[n]
             ring.got(self.base + n, self.at(d, 0), me)
-            ref = self.at(d, 0, n)
-            ring.send(self.base + 2 + n, ref, ref, self.first(-d))
 
         def far1(self):
-            for n in (0, 1):
-                ring.got(self.base + 2 + n, self.at(2, 0, n), me)
+            ring.got(self.base + 2, self.at(2, 0), me)
 
         def send2(self, c):
             di = (0, -1, 1, 2)[c]
             for n, d in ((0, 1), (1, -1)):
                 ring.send(self.base + 4 + 4 * c + n, self.at(di, 0), self.at(di, 0), self.second(d))
+            if c in direct:
+                ring.send(self.base + 6 + 4 * c, self.at(di, 0), self.at(di, 0), self.second(2))
 
         def relay2(self, c):
             di = (0, -1, 1, 2)[c]
             for n, d in ((0, -1), (1, 1)):
                 ring.got(self.base + 4 + 4 * c + n, self.at(di, d), me)
-                ref = self.at(di, d, n)
-                ring.send(self.base + 4 + 4 * c + 2 + n, ref, ref, self.second(-d))
+                if c not in direct:
+                    ref = self.at(di, d, n)
+                    ring.send(self.base + 6 + 4 * c + n, ref, ref, self.second(-d))
 
         def far2(self, c):
             di = (0, -1, 1, 2)[c]
+            if c in direct:
+                return ring.got(self.base + 6 + 4 * c, self.at(di, 2), me)
             for n in (0, 1):
-                ring.got(self.base + 4 + 4 * c + 2 + n, self.at(di, 2, n), me)
+                ring.got(self.base + 6 + 4 * c + n, self.at(di, 2, n), me)
 
     hooks = hooks or {}
     hook = lambda n: [task() for task in hooks.get(n, ())]
@@ -307,20 +311,25 @@
 
 
 def panel_kernel(
-    panels, a_hbm, v_ref, tri_ref, mid_hbm, y_hbm, zh_hbm, zl_hbm,
+    panels, a_hbm, v_hbm, tri_hbm, mid_hbm, y_hbm, zh_hbm, zl_hbm,
     a_mem, ah, al, vbuf, vh, vl, pbuf, cin, rin1, rin2, ytr, colbuf, yrows,
-    packed, summed, gmat, hmat, part, tin1, tin2, tin3, ct, dt, zh, zl, yzh, yzl,
-    a_sem, m_sem, o_sem, z_sem, vs, vr, ys, yr, cols_s, cols_r, hs, hr, cs, cr, zs, zr, ts, tr,
+    packed, summed, gmat, hmat, part, tin1, tin2, tin3, ct, dt, zh, zl, yzh, yzl, tri_ref,
+    a_sem, in_sem, m_sem, o_sem, z_sem, vs, vr, ys, yr, cols_s, cols_r, hs, hr, cs, cr, zs, zr, ts, tr,
 ):
     pos = Place()
     me = pos.dev()
+    own = pos.y * 4 + pos.x
+    v_ref = vbuf.at[own]
     nv, lanes = v_ref.shape
     nb = nv // panels
     rows, cols = a_mem.shape
+    small = (
+        pltpu.make_async_copy(v_hbm, v_ref, in_sem.at[0]), pltpu.make_async_copy(tri_hbm, tri_ref, in_sem.at[1]))
+    for copy in small:
+        copy.start()
     load = pltpu.make_async_copy(a_hbm, a_mem, a_sem)
     load.start()
 
-    vbuf[pos.y * 4 + pos.x] = v_ref[...]
     v_to, v_slot = pos.out_v()
     y_to, y_slot = pos.out_y()
 
@@ -333,6 +342,8 @@
     near += [pos.from_v(), pos.from_y()]
     for dev in near:
         pl.semaphore_signal(barrier, inc=1, device_id=dev, device_id_type=MESH)
+    for copy in small:
+        copy.wait()
     pl.semaphore_wait(barrier, len(near))
 
     def pairs():
@@ -502,7 +513,6 @@
     panels, nb, lanes = reflectors.shape
     nv = panels * nb
     rows, cols = symmetric.shape
-    vmem = pl.BlockSpec(memory_space=pltpu.VMEM)
     anywhere = pl.BlockSpec(memory_space=pl.ANY)
     dma = pltpu.SemaphoreType.DMA
     shape = jax.ShapeDtypeStruct
@@ -511,7 +521,7 @@
         out_shape=(
             shape((rows, cols), F32), shape((16, lanes, nv), F32),
             shape((nv, cols), BF16), shape((nv, cols), BF16)),
-        in_specs=[anywhere, vmem, vmem],
+        in_specs=[pl.BlockSpec(memory_space=pltpu.HBM)] * 3,
         out_specs=(anywhere,) * 4,
         scratch_shapes=[
             pltpu.VMEM((rows, cols), F32),
@@ -534,14 +544,15 @@
             pltpu.VMEM((nv, nv), F32), pltpu.VMEM((nv, nv), F32),
             pltpu.VMEM((nv, cols), BF16), pltpu.VMEM((nv, cols), BF16),
             pltpu.VMEM((nv, cols), BF16), pltpu.VMEM((nv, cols), BF16),
-            dma, dma((4,)), dma((16,)), dma((2,)),
+            pltpu.VMEM(tri_factor.shape, F32),
+            dma, dma((2,)), dma((4,)), dma((16,)), dma((2,)),
             dma((40,)), dma((40,)), dma((40,)), dma((40,)),
             dma((8,)), dma((8,)), dma((20,)), dma((20,)),
             dma((4,)), dma((4,)), dma((4,)), dma((4,)), dma((2,)), dma((2,)),
         ],
         compiler_params=pltpu.CompilerParams(
-            collective_id=0, has_side_effects=True, vmem_limit_bytes=56 * 2**20),
-    )(symmetric, reflectors.reshape(nv, lanes), tri_factor)
+            collective_id=0, has_side_effects=True, vmem_limit_bytes=34 * 2**20),
+    )(*(pltpu.with_memory_space_constraint(v, pltpu.HBM) for v in (symmetric, reflectors.reshape(nv, lanes), tri_factor)))
     tile = 2 * lanes
     return pl.pallas_call(
         product_kernel,
@@ -554,7 +565,7 @@
             pl.BlockSpec((nv, cols), lambda i: (0, 0)),
         ],
         out_specs=pl.BlockSpec((tile, cols), lambda i: (i, 0)),
-        compiler_params=pltpu.CompilerParams(vmem_limit_bytes=58 * 2**20),
+        compiler_params=pltpu.CompilerParams(vmem_limit_bytes=16 * 2**20),
     )(middle, y_rows.reshape(rows, nv), zh, zl)
 
 

time: 92.5 us -> 86.5 us (0.935)
  Pallas kernels: 92.2 us -> 86.4 us
    pallas_call x1, Pallas kernels: 11.6 us -> 6.79 us  [shards(): pl.pallas_call(product_kernel, grid=(rows // tile,), out_shape=shape((row...]
    pallas_call x1, Pallas kernels: 80.6 us -> 79.6 us  [shards(): pl.pallas_call(functools.partial(panel_kernel, panels), out_shape=(shape(...]
where the time goes in v4:
time: 86.5 us; the launch traced here: 86.4 us
  Pallas kernels  86.4 us (100%)
    pallas_call x1, Pallas kernels, shards(): pl.pallas_call(functools.partial(panel_kernel, panels), out_shape=(shape(...  79.6 us
    pallas_call x1, Pallas kernels, shards(): pl.pallas_call(product_kernel, grid=(rows // tile,), out_shape=shape((row...  6.79 us

profile of v4, /device:TPU:1, one launch (start us, length us, event | category | flops | bytes accessed | tf_op | source)
XLA Modules:
  0.0 86.4 jit_solution(9039470836389158267)
XLA Ops:
  0.0 79.6 %shard_map.37 = (f32[2048,1024]{1,0:T(8,128)S(1)}, f32[16,128,256]{2,1,0:T(8,128)S(1)}, bf16[256,1024]{1,0:T(8,128)(2,1)S(1)}, bf16[256,1024]{1,0:T(8,128)(2,1)S(1)}) custom-call(f32[2048,1024]{1,0:T(8,128)} %a_hbm.1, f32[256,128]{1,0:T(8,128)} %bitcast.3, f32[4,64,64]{2,1,0:T(8,128)} %tri_hbm.1), custom_call_target="tpu_custom_call" | custom-call | tf_op jit(solution)/shard_map/pallas_call | solution.py:519
  79.6 6.8 %shard_map.38 = f32[2048,1024]{1,0:T(8,128)} custom-call(f32[2048,1024]{1,0:T(8,128)S(1)} %get-tuple-element.9.mid_ref, f32[2048,256]{1,0:T(8,128)S(1)} %bitcast.2, bf16[256,1024]{1,0:T(8,128)(2,1)S(1)} %get-tuple-element.11.zh, bf16[256,1024]{1,0:T(8,128)(2,1)S(1)} %get-tuple-element.12.zl), custom_call_target="tpu_custom_call" | custom-call | tf_op jit(solution)/shard_map/pallas_call | solution.py:557

commit v5 on v4

--- a/solution.py
+++ b/solution.py
@@ -175,11 +175,11 @@
             h.send2(1 + n)
     hook(1)
     for h in halves:
-        h.relay2(0)
+        h.far1()
+        h.send2(3)
     hook(2)
     for h in halves:
-        h.far1()
-        h.send2(3)
+        h.relay2(0)
     hook(3)
     for c in (1, 2, 3):
         for h in halves:
@@ -354,7 +354,7 @@
             at = pl.ds(pl.multiple_of(i * lanes, lanes), lanes)
             ah[at], al[at] = split(a_mem[at])
 
-    ring_v = plane_gather(pos, vbuf, vs, vr, {1: (pairs,)})
+    ring_v = plane_gather(pos, vbuf, vs, vr, {6: (pairs,)})
     v_done = exchange(v_to, me, v_ref, colbuf.at[v_slot, pl.ds(0, nv)], ts.at[0], tr.at[0])
     for b in range(16):
         high, low = split(vbuf[b])
@@ -506,7 +506,9 @@
 
 
 def product_kernel(mid_ref, y_ref, zh, zl, out_ref):
-    out_ref[...] = mid_ref[...] - dot3(split(y_ref[...]), (zh[...], zl[...]), NN)
+    tile = out_ref.shape[0]
+    at = pl.ds(pl.multiple_of(pl.program_id(0) * tile, tile), tile)
+    out_ref[...] = mid_ref[at] - dot3(split(y_ref[at]), (zh[...], zl[...]), NN)
 
 
 def shards(symmetric, reflectors, tri_factor):
@@ -553,17 +555,13 @@
         compiler_params=pltpu.CompilerParams(
             collective_id=0, has_side_effects=True, vmem_limit_bytes=34 * 2**20),
     )(*(pltpu.with_memory_space_constraint(v, pltpu.HBM) for v in (symmetric, reflectors.reshape(nv, lanes), tri_factor)))
-    tile = 2 * lanes
+    tile = 4 * lanes
+    vmem = pl.BlockSpec(memory_space=pltpu.VMEM)
     return pl.pallas_call(
         product_kernel,
         grid=(rows // tile,),
         out_shape=shape((rows, cols), F32),
-        in_specs=[
-            pl.BlockSpec((tile, cols), lambda i: (i, 0)),
-            pl.BlockSpec((tile, nv), lambda i: (i, 0)),
-            pl.BlockSpec((nv, cols), lambda i: (0, 0)),
-            pl.BlockSpec((nv, cols), lambda i: (0, 0)),
-        ],
+        in_specs=[vmem] * 4,
         out_specs=pl.BlockSpec((tile, cols), lambda i: (i, 0)),
         compiler_params=pltpu.CompilerParams(vmem_limit_bytes=16 * 2**20),
     )(middle, y_rows.reshape(rows, nv), zh, zl)

time: 86.5 us -> 85.1 us (0.984)
  Pallas kernels: 86.4 us -> 85 us
    pallas_call x1, Pallas kernels: 6.79 us -> 5.61 us  [shards(): pl.pallas_call(product_kernel, grid=(rows // tile,), out_shape=shape((row...]
where the time goes in v5:
time: 85.1 us; the launch traced here: 85 us
  Pallas kernels  85 us (100%)
    pallas_call x1, Pallas kernels, shards(): pl.pallas_call(functools.partial(panel_kernel, panels), out_shape=(shape(...  79.4 us
    pallas_call x1, Pallas kernels, shards(): pl.pallas_call(product_kernel, grid=(rows // tile,), out_shape=shape((row...  5.61 us

profile of v5, /device:TPU:1, one launch (start us, length us, event | category | flops | bytes accessed | tf_op | source)
XLA Modules:
  0.0 85.0 jit_solution(12544886641119107838)
XLA Ops:
  0.0 79.4 %shard_map.37 = (f32[2048,1024]{1,0:T(8,128)S(1)}, f32[16,128,256]{2,1,0:T(8,128)S(1)}, bf16[256,1024]{1,0:T(8,128)(2,1)S(1)}, bf16[256,1024]{1,0:T(8,128)(2,1)S(1)}) custom-call(f32[2048,1024]{1,0:T(8,128)} %a_hbm.1, f32[256,128]{1,0:T(8,128)} %bitcast.3, f32[4,64,64]{2,1,0:T(8,128)} %tri_hbm.1), custom_call_target="tpu_custom_call" | custom-call | tf_op jit(solution)/shard_map/pallas_call | solution.py:521
  79.4 5.6 %shard_map.38 = f32[2048,1024]{1,0:T(8,128)} custom-call(f32[2048,1024]{1,0:T(8,128)S(1)} %get-tuple-element.9.mid_ref, f32[2048,256]{1,0:T(8,128)S(1)} %bitcast.2, bf16[256,1024]{1,0:T(8,128)(2,1)S(1)} %get-tuple-element.11.zh, bf16[256,1024]{1,0:T(8,128)(2,1)S(1)} %get-tuple-element.12.zl), custom_call_target="tpu_custom_call" | custom-call | tf_op jit(solution)/shard_map/pallas_call | solution.py:560

commit v6 on v5

--- a/solution.py
+++ b/solution.py
@@ -355,7 +355,6 @@
             ah[at], al[at] = split(a_mem[at])
 
     ring_v = plane_gather(pos, vbuf, vs, vr, {6: (pairs,)})
-    v_done = exchange(v_to, me, v_ref, colbuf.at[v_slot, pl.ds(0, nv)], ts.at[0], tr.at[0])
     for b in range(16):
         high, low = split(vbuf[b])
         vh[:, b * lanes:(b + 1) * lanes] = high
@@ -379,6 +378,7 @@
         cin[i] = cin[i] + pbuf[2 * i + pos.k]
 
     product(0)
+    v_done = exchange(v_to, me, v_ref, colbuf.at[v_slot, pl.ds(0, nv)], ts.at[0], tr.at[0])
     product(1)
     merge(0)
     ring_z.send(0, cin.at[0, pl.ds(0, half)], rin1.at[0], pos.dev(z=right))

time: 85.1 us -> 84.8 us (level)
  no operation moved by 1% of the time
where the time goes in v6:
time: 84.8 us; the launch traced here: 84.7 us
  Pallas kernels  84.7 us (100%)
    pallas_call x1, Pallas kernels, shards(): pl.pallas_call(functools.partial(panel_kernel, panels), out_shape=(shape(...  79.1 us
    pallas_call x1, Pallas kernels, shards(): pl.pallas_call(product_kernel, grid=(rows // tile,), out_shape=shape((row...  5.61 us

profile of v6, /device:TPU:1, one launch (start us, length us, event | category | flops | bytes accessed | tf_op | source)
XLA Modules:
  0.0 84.7 jit_solution(17352643382191382190)
XLA Ops:
  0.0 79.1 %shard_map.37 = (f32[2048,1024]{1,0:T(8,128)S(1)}, f32[16,128,256]{2,1,0:T(8,128)S(1)}, bf16[256,1024]{1,0:T(8,128)(2,1)S(1)}, bf16[256,1024]{1,0:T(8,128)(2,1)S(1)}) custom-call(f32[2048,1024]{1,0:T(8,128)} %a_hbm.1, f32[256,128]{1,0:T(8,128)} %bitcast.3, f32[4,64,64]{2,1,0:T(8,128)} %tri_hbm.1), custom_call_target="tpu_custom_call" | custom-call | tf_op jit(solution)/shard_map/pallas_call | solution.py:521
  79.1 5.6 %shard_map.38 = f32[2048,1024]{1,0:T(8,128)} custom-call(f32[2048,1024]{1,0:T(8,128)S(1)} %get-tuple-element.9.mid_ref, f32[2048,256]{1,0:T(8,128)S(1)} %bitcast.2, bf16[256,1024]{1,0:T(8,128)(2,1)S(1)} %get-tuple-element.11.zh, bf16[256,1024]{1,0:T(8,128)(2,1)S(1)} %get-tuple-element.12.zl), custom_call_target="tpu_custom_call" | custom-call | tf_op jit(solution)/shard_map/pallas_call | solution.py:560
